TPU v7x, 32 devices: a whole 2x2x4 slice. The times are simulated.
32 devices in a mesh: dp: 8 (over z, y), seq: 4 (over x, core).
Axes of the slice: x: 2, y: 2, z: 4, core: 2. Of those that a mesh axis runs over, the one named last changes fastest.
Arguments:
- hidden_in: bfloat16 [32, 1024, 768], P('dp', 'seq'), may hold values from -6 to 6
- time_table: bfloat16 [1024, 128], replicated, may hold values from -6 to 6
- time_step: int32 [32], P('dp'), may hold values from 0 to 1023
- token_pos: int32 [32, 1024], P('dp', 'seq'), may hold values from 0 to 3071, as said below
- heads_weight: bfloat16 [768, 2304], P('seq'), may hold values from -0.15625 to 0.15625
- merge_weight: bfloat16 [768, 768], P('seq'), may hold values from -1.75 to 1.75
- lift_weight: bfloat16 [768, 3072], P('seq'), may hold values from -0.21875 to 0.21875
- lift_bias: bfloat16 [3072], P('seq'), may hold values from -3 to 3
- drop_weight: bfloat16 [3072, 768], P('seq'), may hold values from -0.109375 to 0.109375
- drop_bias: bfloat16 [768], P('seq'), may hold values from -3 to 3
- modulate_weight: bfloat16 [4608, 128], P('seq'), may hold values from -0.5 to 0.5
- modulate_bias: bfloat16 [4608], P('seq'), may hold values from -3 to 3
- first_gain: bfloat16 [768], P('seq'), may hold values from 0.099609375 to 1.8984375
- second_gain: bfloat16 [768], P('seq'), may hold values from 0.099609375 to 1.8984375
- out_grad: bfloat16 [32, 1024, 768], P('dp', 'seq'), may hold values from -6 to 6
Outputs:
- block_out: bfloat16 [32, 1024, 768], P('dp', 'seq')
- input_grad: bfloat16 [32, 1024, 768], P('dp', 'seq')
- heads_grad: float32 [768, 2304], P('seq')
- merge_grad: float32 [768, 768], P('seq')
- lift_grad: float32 [768, 3072], P('seq')
- liftbias_grad: float32 [3072], P('seq')
- drop_grad: float32 [3072, 768], P('seq')
- dropbias_grad: float32 [768], P('seq')
- modulate_grad: float32 [4608, 128], P('seq')
- modulatebias_grad: float32 [4608], P('seq')
- firstgain_grad: float32 [768], P('seq')
- secondgain_grad: float32 [768], P('seq')
- table_grad: float32 [1024, 128], P('seq')
Inputs may be any that keep to these rules, and one draw needn't show every extreme that they name: `token_pos`: positions count up by one along a row and start again at 0 at each separator token; in every aligned group of 4 rows one row holds no separator; such a row in the first group starts at 2048, such a row in the second group starts at 0.
All inputs are finite; a program needn't handle non-finite values.
Results may differ from a plain program's by a relative error of at most 0.017.
The roundings to bfloat16 on the way count: a program that leaves them out, or rounds other values in their place, can miss the bound.
Values may be sent and summed in bfloat16 or wider, within the bound.
No kernel may reach another device: no remote copies, remote signals or barrier semaphores. Data moves between devices by JAX's collectives and lax.ppermute only.
A program may use at most 320 MiB of HBM per device.

v0:
```python
from functools import partial
import math

import jax
import jax.numpy as jnp
from jax import lax
from jax.experimental import pallas as pl
from jax.experimental.pallas import tpu as pltpu
from jax.sharding import PartitionSpec as P

HEADS = 12
EPSILON = 1e-05
LANES = 128
VMEM = 60 * 1024 * 1024
LOW = jnp.bfloat16
FULL = jnp.float32


def matmul(left, right, left_dim=1, right_dim=0):
    dims = (((left_dim,), (right_dim,)), ((), ()))
    return lax.dot_general(left, right, dims, preferred_element_type=FULL)


def call(body, name, grid, in_specs, out_specs, out_shape, scratch, flops, args, moved):
    return pl.pallas_call(
        body,
        name=name,
        grid_spec=pltpu.PrefetchScalarGridSpec(
            num_scalar_prefetch=1,
            grid=grid,
            in_specs=in_specs,
            out_specs=out_specs,
            scratch_shapes=scratch,
        ),
        out_shape=out_shape,
        compiler_params=pltpu.CompilerParams(
            dimension_semantics=("arbitrary",) * len(grid), vmem_limit_bytes=VMEM
        ),
        cost_estimate=pl.CostEstimate(flops=flops, bytes_accessed=moved, transcendentals=0)
        if name in ("feed", "two", "add")
        else pl.CostEstimate(flops=1024, bytes_accessed=1024, transcendentals=0),
    )(*args)


def whole(shape):
    zeros = (0,) * len(shape)
    return pl.BlockSpec(shape, lambda *_: zeros, pipeline_mode=pl.Buffered(1))


def kept(shape):
    zeros = (0,) * len(shape)
    return pl.BlockSpec(shape, lambda *_: zeros)


def assemble(at, target, pieces, start, blocks):
    me, b = at[0], at[1]
    own, core, across, handed, core_across, core_handed = pieces
    rows = target.shape[0] // 8
    width = target.shape[1] // blocks
    halves = (
        (me, 0, lambda cut: own[0, cut, :]),
        (me, 1, lambda cut: own[1, cut, :]),
        (me ^ 1, 0, lambda cut: core[0, cut, :]),
        (me ^ 1, 1, lambda cut: core[1, cut, :]),
        (me ^ 2, b, lambda cut: across[cut, :]),
        (me ^ 2, 1 - b, lambda cut: handed[cut, :]),
        (me ^ 3, b, lambda cut: core_across[cut, :]),
        (me ^ 3, 1 - b, lambda cut: core_handed[cut, :]),
    )
    for shard, half, read in halves:
        place = pl.ds(pl.multiple_of((2 * shard + half) * rows, 16), rows)
        for k in range(blocks):
            cut = slice(start + k * rows, start + (k + 1) * rows)
            target[place, k * width : (k + 1) * width] = read(cut)


def portion(pieces, start, size):
    at = start // size
    return [
        pl.BlockSpec(
            p.shape[:-2] + (size, p.shape[-1]),
            partial(lambda n, *_: (0,) * n + (at, 0), len(p.shape) - 2),
            pipeline_mode=pl.Buffered(1),
        )
        for p in pieces
    ]


def split_rows(me, value, keep, send):
    rows = value.shape[0] // 4
    mine_x, mine_c = me >> 1, me & 1
    for j in range(4):
        part = value[j * rows : (j + 1) * rows].astype(LOW)[None]
        at = (j >> 1) ^ mine_x

        @pl.when(mine_c == (j & 1))
        def _(part=part, at=at):
            keep[pl.ds(at, 1)] = part

        @pl.when(mine_c != (j & 1))
        def _(part=part, at=at):
            send[pl.ds(at, 1)] = part


def normalize(values):
    center = values - jnp.mean(values, axis=-1, keepdims=True)
    inverse = lax.rsqrt(jnp.mean(center * center, axis=-1, keepdims=True) + EPSILON)
    return center * inverse, inverse


def unnormalize(weighted, unit, inverse):
    first = jnp.mean(weighted, axis=-1, keepdims=True)
    second = jnp.mean(weighted * unit, axis=-1, keepdims=True)
    return inverse * (weighted - first - unit * second)


def lower_half(head):
    lane = lax.broadcasted_iota(jnp.int32, (1, LANES), 1)
    return (lane & (head - 1)) < head // 2


def column_sum(values):
    return jnp.sum(values, axis=0, keepdims=True)


def project_kernel(head, me_ref, hidden, vectors, p0, p1, p2, p3, p4, p5, cosine, sine, turned, query, key, value, weight):
    @pl.when(pl.program_id(0) == 0)
    def _():
        assemble(me_ref, weight, (p0, p1, p2, p3, p4, p5), 0, 3)

    unit, _ = normalize(hidden[...].astype(FULL))
    low = (unit * vectors[0:1, :] * vectors[1:2, :] + vectors[2:3, :]).astype(LOW)
    turned[...] = low.T
    width = low.shape[1]
    cos, sin = cosine[...], sine[...]
    under = lower_half(head)
    signed = jnp.where(under, -sin, sin)
    scale = 1.0 / math.sqrt(head)
    for which, target in enumerate((query, key)):
        part = matmul(low, weight[:, which * width : (which + 1) * width])
        for j in range(width // LANES):
            block = part[:, j * LANES : (j + 1) * LANES]
            turned = jnp.where(
                under,
                pltpu.roll(block, LANES - head // 2, 1),
                pltpu.roll(block, head // 2, 1),
            )
            turned = (block * cos + turned * signed).astype(LOW)
            if which == 0:
                turned = turned * jnp.asarray(scale, LOW)
            target[:, j * LANES : (j + 1) * LANES] = turned
    value[...] = matmul(low, weight[:, 2 * width :]).astype(LOW)


def project(me, hidden, vectors, pieces, cosine, sine, head):
    length, width = hidden.shape
    step = 512
    rows = pl.BlockSpec((step, width), lambda i, _: (i, 0))
    angle = pl.BlockSpec((step, LANES), lambda i, _: (i, 0))
    out = jax.ShapeDtypeStruct((length, width), LOW)
    return call(
        partial(project_kernel, head),
        "project",
        (length // step,),
        [rows, whole(vectors.shape)] + portion(pieces, 0, 3 * width // 8) + [angle, angle],
        [pl.BlockSpec((width, step), lambda i, _: (0, i))] + [rows] * 3,
        [jax.ShapeDtypeStruct((width, length), LOW)] + [out] * 3,
        [pltpu.VMEM((width, 3 * width), LOW)],
        2 * length * width * 3 * width,
        (me, hidden, vectors, *pieces, cosine, sine),
        2 * length * width * 8,
    )


def attend_kernel(step, head, me_ref, query, key, value, mixed, logsum):
    lane = lax.broadcasted_iota(jnp.int32, (1, LANES), 1)
    first = lane < head
    keys, values = key[...], value[...]
    zero = jnp.zeros_like(keys)
    split = (jnp.where(first, keys, zero), jnp.where(first, zero, keys))
    for i in range(query.shape[0] // step):
        at = slice(i * step, (i + 1) * step)
        block = query[at, :]
        outs, sums = [], []
        for h in range(2):
            scores = matmul(block, split[h], 1, 1)
            peak = jnp.max(scores, axis=1, keepdims=True)
            expos = jnp.exp(scores - peak)
            total = jnp.sum(expos, axis=1, keepdims=True)
            outs.append(matmul(expos.astype(LOW), values) * (1.0 / total))
            sums.append(peak + jnp.log(total))
        mixed[at, :] = jnp.where(first, outs[0], outs[1]).astype(LOW)
        turned = jnp.where(first, sums[0], sums[1]).T
        logsum[0, 0:1, at] = turned[0:1, :]
        logsum[0, 1:2, at] = turned[head : head + 1, :]


def attend(me, query, key, value, head):
    length, width = query.shape
    pairs = width // LANES
    block = pl.BlockSpec((length, LANES), lambda i, _: (0, i))
    return call(
        partial(attend_kernel, 512, head),
        "attend",
        (pairs,),
        [block] * 3,
        [block, pl.BlockSpec((1, 2, length), lambda i, _: (i, 0, 0))],
        [
            jax.ShapeDtypeStruct((length, width), LOW),
            jax.ShapeDtypeStruct((pairs, 2, length), FULL),
        ],
        [],
        16 * length * length * width,
        (me, query, key, value),
        2 * length * width * 4,
    )


def merge_kernel(me_ref, mixed, hidden, vectors, p0, p1, p2, p3, p4, p5, middle, adapted, weight):
    @pl.when(pl.program_id(0) == 0)
    def _():
        assemble(me_ref, weight, (p0, p1, p2, p3, p4, p5), 0, 1)

    branch = matmul(mixed[...], weight[...])
    mid = hidden[...].astype(FULL) + vectors[0:1, :] * branch
    middle[...] = mid
    unit, _ = normalize(mid)
    adapted[...] = (unit * vectors[1:2, :] * vectors[2:3, :] + vectors[3:4, :]).astype(LOW)


def merge(me, mixed, hidden, vectors, pieces):
    length, width = hidden.shape
    step = 512
    rows = pl.BlockSpec((step, width), lambda i, _: (i, 0))
    return call(
        merge_kernel,
        "merge",
        (length // step,),
        [rows, rows, whole(vectors.shape)] + portion(pieces, 3 * width // 8, width // 8),
        [rows, rows],
        [jax.ShapeDtypeStruct((length, width), FULL), jax.ShapeDtypeStruct((length, width), LOW)],
        [pltpu.VMEM((width, width), LOW)],
        2 * length * width * width,
        (me, mixed, hidden, vectors, *pieces),
        2 * length * width * 6,
    )


def feed_kernel(last, at_ref, adapted, upstream, vectors, lift_bias, p0, p1, p2, p3, *refs):
    if last:
        low_in, grad_in, middle, o0, o1, o2, o3, adapted_grad, sums, liftbias_grad, keep, send = refs[:12]
        grads, pack, lift, turned, lowered_grad, out_sem, lowered, low_got, grad_got, middle_got, sem = refs[12:]
        copies = [
            pltpu.make_async_copy(source, target, sem.at[k])
            for k, (source, target) in enumerate(
                ((low_in, low_got), (grad_in, grad_got), (middle, middle_got))
            )
        ]
        for copy in copies:
            copy.start()
    else:
        lowered, adapted_grad, liftbias_grad, keep, send = refs[:5]
        grads, pack, lift, turned, lowered_grad, out_sem = refs[5:]
    for d, piece in enumerate((p0, p1, p2, p3)):
        pack[pl.ds(at_ref[0] ^ d, 1)] = piece[...][None]
    me = at_ref[0]
    gate = vectors[0:1, :]
    rows = lift.shape[0] // 4
    step = lift.shape[1] // 2

    def leave(j, half):
        at = slice(0, step) if half == 0 else slice(step + (half - 1) * rows, step + half * rows)
        where = (j >> 1) ^ (me >> 1)
        for target, odd in ((keep, 0), (send, 1)):

            @pl.when(((me ^ j) & 1) == odd)
            def _(target=target):
                pltpu.make_async_copy(
                    grads.at[j, at, :], target.at[where, at, :], out_sem.at[j, half]
                ).start()

    def left(j, half):
        at = slice(0, step) if half == 0 else slice(step + (half - 1) * rows, step + half * rows)
        pltpu.make_async_copy(
            grads.at[j, at, :], keep.at[0, at, :], out_sem.at[j, half]
        ).wait()

    turned[...] = adapted[...].T
    lowered_grad[...] = (gate * upstream[...].astype(FULL)).astype(LOW)
    for i in range(2):
        deep = slice(step + i * rows, step + (i + 1) * rows)
        for j in range(4):
            lift[j * rows : (j + 1) * rows, :] = pack[j, deep, :]
        weight_up = lift[...]
        weight_down = jnp.concatenate([pack[2 * i, :step, :], pack[2 * i + 1, :step, :]], axis=0)
        across = slice(2 * i * step, 2 * (i + 1) * step)
        upper = matmul(adapted[...], weight_up) + lift_bias[:, across]
        square = upper * upper
        root = math.sqrt(2.0 / math.pi)
        bent = jnp.tanh(upper * (root + root * 0.044715 * square))
        half = 0.5 + 0.5 * bent
        slope = half + upper * (0.5 - 0.5 * bent * bent) * (root + 3.0 * root * 0.044715 * square)
        active = (upper * half).astype(LOW)
        low_part = matmul(active, weight_down)
        down = lowered_grad[...]
        upper_grad = (matmul(down, weight_down, 1, 1) * slope).astype(LOW)
        grad_part = matmul(upper_grad, weight_up, 1, 1)
        if i == 0:
            lowered[...] = low_part
            adapted_grad[...] = grad_part
        else:
            lowered[...] += low_part
            adapted_grad[...] += grad_part
        liftbias_grad[:, across] = column_sum(upper_grad.astype(FULL))
        drop_part = matmul(active, down, 0, 0).astype(LOW)
        for k in range(2):
            grads[2 * i + k, :step, :] = drop_part[k * step : (k + 1) * step]
            leave(2 * i + k, 0)
        lift_part = matmul(turned[...], upper_grad).astype(LOW)
        for j in range(4):
            grads[j, deep, :] = lift_part[j * rows : (j + 1) * rows]
            leave(j, 1 + i)

    if last:
        for copy in copies:
            copy.wait()
        adapted_grad[...] += grad_got[...]
        total = lowered[...] + low_got[...] + vectors[1:2, :]
        low_got[...] = middle_got[...] + gate * total
        span = o0.shape[0]
        for d, target in enumerate((o0, o1, o2, o3)):
            target[...] = low_got[pl.ds(pl.multiple_of((me ^ d) * span, 16), span), :].astype(LOW)
        sums[0:1, :] = column_sum(upstream[...].astype(FULL) * total)
        sums[1:2, :] = column_sum(lowered_grad[...].astype(FULL))
    for j in range(4):
        for half in range(3):
            left(j, half)


def feed(me, adapted, upstream, vectors, lift_bias, pieces, before=()):
    length, width = adapted.shape
    last = len(before) > 0
    units = lift_bias.shape[1]
    wide = jax.ShapeDtypeStruct((length, width), FULL)
    low = jax.ShapeDtypeStruct((length // 4, width), LOW)
    more = jax.ShapeDtypeStruct((2, units // 2, width), LOW)
    sums = jax.ShapeDtypeStruct((8, width), FULL)
    bias = jax.ShapeDtypeStruct((1, units), FULL)
    outs = [low] * 4 + [wide, sums, bias, more, more] if last else [wide, wide, bias, more, more]
    scratch = [
        pltpu.VMEM((4, units // 2, width), LOW),
        pltpu.VMEM((4, units // 2, width), LOW),
        pltpu.VMEM((width, units // 2), LOW),
        pltpu.VMEM((width, length), LOW),
        pltpu.VMEM((length, width), LOW),
        pltpu.SemaphoreType.DMA((4, 3)),
    ]
    if last:
        scratch += [pltpu.VMEM((length, width), FULL)] * 4 + [pltpu.SemaphoreType.DMA((3,))]
    return call(
        partial(feed_kernel, last),
        "feed",
        (1,),
        [whole(a.shape) for a in (adapted, upstream, vectors, lift_bias, *pieces)]
        + [pl.BlockSpec(memory_space=pl.ANY) for _ in before],
        [whole(o.shape) for o in outs[:-2]] + [pl.BlockSpec(memory_space=pl.ANY)] * 2,
        outs,
        scratch,
        12 * length * width * units,
        (me, adapted, upstream, vectors, lift_bias, *pieces, *before),
        8 * width * units + 24 * length * width,
    )


def unmerge_kernel(
    me_ref, adapted_grad, middle, upstream, mixed, vectors, p0, p1, p2, p3, p4, p5,
    middle_grad, mixed_grad, sums, keep, send, weight, total,
):
    i = pl.program_id(0)

    @pl.when(i == 0)
    def _():
        assemble(me_ref, weight, (p0, p1, p2, p3, p4, p5), 0, 1)
        total[...] = jnp.zeros_like(total)
        sums[...] = jnp.zeros_like(sums)

    gate, gain, grow = vectors[0:1, :], vectors[1:2, :], vectors[2:3, :]
    unit, inverse = normalize(middle[...])
    grad = adapted_grad[...]
    sums[0:1, :] += column_sum(grad)
    sums[1:2, :] += column_sum(grad * (unit * gain))
    normed_grad = grad * grow
    sums[2:3, :] += column_sum(normed_grad * unit)
    mid_grad = upstream[...].astype(FULL) + unnormalize(normed_grad * gain, unit, inverse)
    middle_grad[...] = mid_grad
    low = mixed[...]
    sums[3:4, :] += column_sum(mid_grad * matmul(low, weight[...]))
    branch_grad = (gate * mid_grad).astype(LOW)
    total[...] += matmul(low, branch_grad, 0, 0)
    mixed_grad[...] = matmul(branch_grad, weight[...], 1, 1).astype(LOW)

    @pl.when(i == pl.num_programs(0) - 1)
    def _():
        split_rows(me_ref[0], total[...], keep, send)


def unmerge(me, adapted_grad, middle, upstream, mixed, vectors, pieces):
    length, width = middle.shape
    step = 512
    rows = pl.BlockSpec((step, width), lambda i, _: (i, 0))
    part = (2, width // 4, width)
    return call(
        unmerge_kernel,
        "unmerge",
        (length // step,),
        [rows] * 4 + [whole(vectors.shape)] + portion(pieces, 3 * width // 8, width // 8),
        [rows, rows, kept((8, width)), kept(part), kept(part)],
        [
            jax.ShapeDtypeStruct((length, width), FULL),
            jax.ShapeDtypeStruct((length, width), LOW),
            jax.ShapeDtypeStruct((8, width), FULL),
            jax.ShapeDtypeStruct(part, LOW),
            jax.ShapeDtypeStruct(part, LOW),
        ],
        [pltpu.VMEM((width, width), LOW), pltpu.VMEM((width, width), FULL)],
        6 * length * width * width,
        (me, adapted_grad, middle, upstream, mixed, vectors, *pieces),
        2 * length * width * 12,
    )


def unattend_kernel(step, head, sums, me_ref, query, key, value, mixed, mixed_grad, logsum, cosine, sine, *refs):
    if sums:
        grads, mine, other = refs[2:5]
        mine[...] = plus(refs[0][0], refs[1][0])
        other[...] = plus(refs[0][1], refs[1][1])
    else:
        grads = refs[0]
    query_sum, key_sum, value_sum = refs[-3:]
    lane = lax.broadcasted_iota(jnp.int32, (1, LANES), 1)
    first = lane < head
    keys, values = key[...], value[...]
    zero = jnp.zeros_like(keys)
    keys_h = (jnp.where(first, keys, zero), jnp.where(first, zero, keys))
    values_h = (jnp.where(first, values, zero), jnp.where(first, zero, values))
    turned = keys.T
    scale = 1.0 / math.sqrt(head)
    for i in range(query.shape[0] // step):
        at = slice(i * step, (i + 1) * step)
        block, grad = query[at, :], mixed_grad[at, :]
        product = (grad.astype(FULL) * mixed[at, :].astype(FULL)).T
        queries, values_new, keys_new = [], [], []
        for h in range(2):
            center = jnp.sum(product[h * head : (h + 1) * head], axis=0, keepdims=True)
            probs = jnp.exp(matmul(keys_h[h], block, 1, 1) - logsum[0, h : h + 1, at])
            probs_grad = matmul(values_h[h], grad, 1, 1)
            scores_grad = (probs * (probs_grad - center)).astype(LOW)
            values_new.append(matmul(probs.astype(LOW), grad))
            keys_new.append(matmul(scores_grad, block))
            queries.append(matmul(turned[h * head : (h + 1) * head], scores_grad))
        query_sum[at, :] = jnp.concatenate(queries, axis=0).T * scale
        key_part = jnp.where(first, keys_new[0], keys_new[1])
        value_part = jnp.where(first, values_new[0], values_new[1])
        if i == 0:
            key_sum[...] = key_part
            value_sum[...] = value_part
        else:
            key_sum[...] += key_part
            value_sum[...] += value_part
    under = lower_half(head)
    cos, sin = cosine[...], sine[...]
    for which, total in enumerate((query_sum, key_sum)):
        rotated = total[...]
        swept = rotated * sin
        back = jnp.where(
            under, pltpu.roll(swept, LANES - head // 2, 1), -pltpu.roll(swept, head // 2, 1)
        )
        grads[which] = (rotated * cos + back).astype(LOW)
    grads[2] = value_sum[...].astype(LOW)


def unattend(
    me, query, key, value, mixed, mixed_grad, logsum, cosine, sine, head, start, pairs, sums=()
):
    length = mixed.shape[0]
    width = pairs * LANES
    more, outs, specs = [], [], []
    if sums:
        _, rows, columns = sums[0].shape
        part = rows // pairs
        more = [pl.BlockSpec((2, part, columns), lambda i, _: (0, i, 0))] * 2
        outs = [jax.ShapeDtypeStruct((rows, columns), LOW)] * 2
        specs = [pl.BlockSpec((part, columns), lambda i, _: (i, 0))] * 2
    block = pl.BlockSpec((length, LANES), lambda i, _: (0, i + start))
    own = pl.BlockSpec((length, LANES), lambda i, _: (0, i))
    return call(
        partial(unattend_kernel, 256, head, len(sums)),
        "unattend",
        (pairs,),
        [block] * 5
        + [pl.BlockSpec((1, 2, length), lambda i, _: (i + start, 0, 0))]
        + [whole((length, LANES))] * 2
        + more,
        [pl.BlockSpec((3, length, LANES), lambda i, _: (0, 0, i))] + specs,
        [jax.ShapeDtypeStruct((3, length, width), LOW)] + outs,
        [pltpu.VMEM((length, LANES), FULL)] * 3,
        40 * length * length * width,
        (me, query, key, value, mixed, mixed_grad, logsum, cosine, sine, *sums),
        2 * length * width * 8,
    )


def weigh_kernel(riders, sums, me_ref, turned, grads, *refs):
    ins, outs = refs[: riders + sums], refs[riders + sums :]
    keep, send = outs[:2]
    outs = outs[2:]
    if sums:
        mine, other = outs[:2]
        outs = outs[2:]
    found, sem = outs[:2]
    outs = outs[2:]
    me = me_ref[0]
    rows, wide = found.shape[1:]
    step = grads.shape[2]
    moves = []
    if riders:
        for k, (source, target) in enumerate(((ins[0], keep), (ins[1], send))):
            at = target.at[:, :, wide : wide + source.shape[2]]
            moves.append(pltpu.make_async_copy(source, at, sem.at[4 + k, 0]))
    if sums:
        for k in range(2):
            moves.append(pltpu.make_async_copy(ins[riders + k], outs[k], sem.at[4 + k, 1]))
    for move in moves:
        move.start()
    for which in range(3):
        cut = slice(which * step, (which + 1) * step)
        value = matmul(turned[...], grads[which]).astype(LOW)
        for j in range(4):
            found[j, :, cut] = value[j * rows : (j + 1) * rows]
            where = (j >> 1) ^ (me >> 1)
            for target, odd in ((keep, 0), (send, 1)):

                @pl.when(((me ^ j) & 1) == odd)
                def _(target=target, j=j, cut=cut, which=which, where=where):
                    pltpu.make_async_copy(
                        found.at[j, :, cut], target.at[where, :, cut], sem.at[j, which]
                    ).start()

    for move in moves:
        move.wait()
    if sums:
        mine[...] = plus(outs[0][0], outs[1][0])
        other[...] = plus(outs[0][1], outs[1][1])
    for j in range(4):
        for which in range(3):
            cut = slice(which * step, (which + 1) * step)
            pltpu.make_async_copy(
                found.at[j, :, cut], keep.at[0, :, cut], sem.at[j, which]
            ).wait()


def weigh(me, turned, grads, riders=(), sums=()):
    width, length = turned.shape
    step = grads.shape[2]
    more = riders[0].shape[2] if riders else 0
    shape = jax.ShapeDtypeStruct((2, width // 4, 3 * step + more), LOW)
    outs, scratch = [shape, shape], []
    away = pl.BlockSpec(memory_space=pl.ANY)
    specs = [away, away]
    if sums:
        out = jax.ShapeDtypeStruct(sums[0].shape[1:], LOW)
        outs += [out, out]
        specs += [whole(out.shape)] * 2
        scratch = [pltpu.VMEM(sums[0].shape, LOW)] * 2
    return call(
        partial(weigh_kernel, len(riders), len(sums)),
        "weigh",
        (1,),
        [whole(a.shape) for a in (turned, grads, *riders)] + [away] * len(sums),
        specs,
        outs,
        [pltpu.VMEM((4, width // 4, 3 * step), LOW), pltpu.SemaphoreType.DMA((6, 3))] + scratch,
        6 * length * width * step,
        (me, turned, grads, *riders, *sums),
        2 * length * width * 7,
    )


def unproject_kernel(me_ref, g0, g1, hidden, middle_grad, vectors, p0, p1, p2, p3, p4, p5, o0, o1, o2, o3, sums, weight):
    i = pl.program_id(0)

    @pl.when(i == 0)
    def _():
        assemble(me_ref, weight, (p0, p1, p2, p3, p4, p5), 0, 3)
        sums[...] = jnp.zeros_like(sums)

    gain, grow = vectors[0:1, :], vectors[1:2, :]
    width = hidden.shape[1]
    grad, at = None, 0
    for part in (g0, g1):
        size = part.shape[2]
        for which in range(3):
            low = which * width + at
            term = matmul(part[which], weight[:, low : low + size], 1, 1)
            grad = term if grad is None else grad + term
        at += size
    unit, inverse = normalize(hidden[...].astype(FULL))
    sums[0:1, :] += column_sum(grad)
    sums[1:2, :] += column_sum(grad * (unit * gain))
    normed_grad = grad * grow
    sums[2:3, :] += column_sum(normed_grad * unit)
    low = (middle_grad[...] + unnormalize(normed_grad * gain, unit, inverse)).astype(LOW)
    for d, target in enumerate((o0, o1, o2, o3)):

        @pl.when(i == me_ref[0] ^ d)
        def _(target=target):
            target[...] = low


def unproject(me, grads, hidden, middle_grad, vectors, pieces):
    length, width = hidden.shape
    step = length // 4
    rows = pl.BlockSpec((step, width), lambda i, _: (i, 0))
    return call(
        unproject_kernel,
        "unproject",
        (length // step,),
        [pl.BlockSpec((3, step, g.shape[2]), lambda i, _: (0, i, 0)) for g in grads]
        + [rows, rows, whole(vectors.shape)]
        + portion(pieces, 0, 3 * width // 8),
        [kept((step, width))] * 4 + [kept((8, width))],
        [jax.ShapeDtypeStruct((step, width), LOW)] * 4 + [jax.ShapeDtypeStruct((8, width), FULL)],
        [pltpu.VMEM((width, 3 * width), LOW)],
        6 * length * width * width,
        (me, *grads, hidden, middle_grad, vectors, *pieces),
        2 * length * width * 10,
    )


def lay_kernel(me_ref, *refs):
    for d, part in enumerate(refs[:-1]):
        refs[-1][pl.ds(me_ref[0] ^ d, 1)] = part[...][None]


def lay(me, parts):
    shape = (len(parts),) + parts[0].shape
    return call(
        lay_kernel, "lay", (1,), [whole(p.shape) for p in parts], [whole(shape)],
        [jax.ShapeDtypeStruct(shape, LOW)], [], 1024, (me, *parts), 1024,
    )[0]


def finish_kernel(
    seqs, columns, depth, me_ref, parts, others, heads, merges, modulate, modulate_bias, up, down, one, two, table
):
    half, rows = parts.shape[0], parts.shape[1] - 8
    size = 2 * half
    wide = parts.shape[2] // 2
    width = merges.shape[1]
    part = width // 2
    for p in range(size):
        at = slice(p * rows, (p + 1) * rows)
        value = jnp.where(
            me_ref[1] == p // half, parts[p % half, 8:, :], others[p % half, 8:, :]
        ).astype(FULL)
        for k in range(3):
            heads[at, k * width : k * width + part] = value[:, k * part : (k + 1) * part]
            heads[at, k * width + part : (k + 1) * width] = value[:, (5 + k) * part : (6 + k) * part]
        merges[at, :] = value[:, 3 * part : 5 * part]
    small = jnp.concatenate(
        [
            source[p, :8, :wide].astype(FULL) + source[p, :8, wide:].astype(FULL)
            for source in (parts, others)
            for p in range(half)
        ],
        axis=0,
    )
    row = lax.broadcasted_iota(jnp.int32, (8 * size, 1), 0) & 7
    mine = row < seqs
    zero = jnp.zeros((), FULL)
    grads = jnp.where(mine, small[:, :columns], zero)
    conds = jnp.where(mine, small[:, columns : columns + depth], zero)
    conds_grad = jnp.where(mine, small[:, columns + depth : columns + 2 * depth], zero)
    steps = small[:, columns + 2 * depth : columns + 2 * depth + 1].astype(jnp.int32)

    def exact(left, right):
        dims = (((0,), (0,)), ((), ()))
        return lax.dot_general(
            left, right, dims, precision=lax.Precision.HIGHEST, preferred_element_type=FULL
        )

    modulate[...] = exact(grads, conds)
    modulate_bias[...] = column_sum(grads)[0]
    ends = column_sum(jnp.where(row == seqs, small, zero))
    at = 0
    for target in (up, down, one, two):
        size = target.shape[0]
        target[...] = ends[0, at : at + size]
        at += size
    share = table.shape[0]
    own = me_ref[0] * share + lax.broadcasted_iota(jnp.int32, (1, share), 1)
    table[...] = exact(jnp.where(mine & (steps == own), 1.0, 0.0), conds_grad)


def finish(me, parts, others, width, columns, depth, sizes, share):
    shapes = [(width // 4, 3 * width), (width // 4, width), (columns, depth), (columns,)]
    shapes += [(size,) for size in sizes] + [(share, depth)]
    return call(
        partial(finish_kernel, 4, columns, depth), "finish", (1,), [whole(parts.shape)] * 2,
        [whole(s) for s in shapes], [jax.ShapeDtypeStruct(s, FULL) for s in shapes], [], 1024,
        (me, parts, others), 1024,
    )


def swap(array, axis, distance):
    size = lax.axis_size(axis)
    return lax.ppermute(array, axis, [(i, i ^ distance) for i in range(size)])


def fence(*trees):
    return lax.optimization_barrier(trees)


def bit(axis, distance):
    return (lax.axis_index(axis) // distance) % 2


def choose(parts, at):
    return lax.dynamic_index_in_dim(parts, at, 0, keepdims=False)


def choose_all(array, place):
    count = array.shape[0]
    return jnp.stack([choose(array, place ^ k) for k in range(count)])


def payload(parts):
    return jnp.concatenate([p.reshape(2, p.shape[0] // 2, p.shape[1]) for p in parts], axis=1)


def blocks_of(weight, width):
    return [weight[:, k : k + width] for k in range(0, weight.shape[1], width)]


def powers(size):
    return [1 << k for k in range(size.bit_length() - 1)]


def plus(*terms):
    total = terms[0].astype(FULL)
    for term in terms[1:]:
        total = total + term.astype(FULL)
    return total.astype(LOW)


def other_kernel(at_ref, kept_term, got, other):
    other[...] = plus(kept_term[0], got[0])


def sum_other(kept_term, got):
    _, rows, columns = kept_term.shape
    steps = 4 if rows % 256 == 0 else 2
    part = rows // steps
    two = pl.BlockSpec((1, part, columns), lambda i, _: (1, i, 0))
    return call(
        other_kernel, "other", (steps,), [two, two], [pl.BlockSpec((part, columns), lambda i, _: (i, 0))],
        [jax.ShapeDtypeStruct((rows, columns), LOW)], [], 1024,
        (jnp.zeros((1,), jnp.int32), kept_term, got), 1024,
    )[0]


def three_kernel(at_ref, kept_term, got, last, total):
    total[...] = plus(kept_term[0], got[0], last[...])


def sum_three(kept_term, got, last):
    _, rows, columns = kept_term.shape
    part = rows // 2
    two = pl.BlockSpec((1, part, columns), lambda i, _: (0, i, 0))
    one = pl.BlockSpec((part, columns), lambda i, _: (i, 0))
    return call(
        three_kernel, "two", (2,), [two, two, one], [one],
        [jax.ShapeDtypeStruct((rows, columns), LOW)], [], 1 << 33,
        (jnp.zeros((1,), jnp.int32), kept_term, got, last), 1 << 24,
    )[0]


def two_kernel(at_ref, first, second, total):
    total[...] = plus(first[...], second[...])


def sum_two(first, second):
    rows, columns = first.shape
    steps = 2 if rows % 32 == 0 else 1
    spec = pl.BlockSpec((rows // steps, columns), lambda i, _: (i, 0))
    return call(
        two_kernel, "two", (steps,), [spec] * 2, [spec],
        [jax.ShapeDtypeStruct((rows, columns), LOW)], [], 1 << 33,
        (jnp.zeros((1,), jnp.int32), first, second), 1 << 24,
    )[0]


def beside_kernel(at_ref, a, b, c, d, e, mine, other):
    cut = a.shape[2]
    for target, at in ((mine, at_ref[0]), (other, 1 - at_ref[0])):
        at = pl.ds(at, 1)
        target[:, :cut] = plus(a[at], b[at])[0]
        target[:, cut:] = plus(c[0, at], d[0, at], e[at])[0]


def split_beside(first, second):
    args = [a.reshape(a.shape[:-2] + (2, -1, a.shape[-1])) for a in (*first, *second)]
    rows = args[0].shape[1]
    out = (rows, args[0].shape[2] + args[4].shape[2])
    pair = pl.BlockSpec((1,) + args[2].shape[1:], lambda *_: (0, 0, 0, 0), pipeline_mode=pl.Buffered(1))
    return call(
        beside_kernel, "beside", (1,),
        [whole(args[0].shape), whole(args[1].shape), pair, pair, whole(args[4].shape)], [whole(out)] * 2,
        [jax.ShapeDtypeStruct(out, LOW)] * 2, [], 1024, (place_of(1), *args), 1024,
    )


def terms_kernel(at_ref, small, parts, total):
    value = plus(*[parts[k] for k in range(parts.shape[0])])
    for k in range(total.shape[0]):
        total[k, :8, :] = small[...]
        total[k, 8:, :] = value


def gather_terms(small, parts):
    shape = (parts.shape[0], 8 + parts.shape[1], small.shape[1])
    return call(
        terms_kernel, "terms", (1,), [whole(small.shape), whole(parts.shape)], [whole(shape)],
        [jax.ShapeDtypeStruct(shape, LOW)], [], 1024, (jnp.zeros((1,), jnp.int32), small, parts), 1024,
    )[0]


def exchange(parts):
    size = lax.axis_size("dp")
    groups = None
    if parts.shape[0] < size:
        groups = [list(range(b, size, 2)) for b in range(2)]
    return lax.all_to_all(parts, "dp", 0, 0, axis_index_groups=groups, tiled=True)


def deal(term, size=None):
    size = size or lax.axis_size("dp")
    rows, columns = term.shape
    return exchange(term.reshape(size, rows // size, columns))


def add_kernel(at_ref, parts, total):
    total[...] = plus(*[parts[k] for k in range(parts.shape[0])])


def add_up(parts):
    shape = parts.shape[1:]
    return call(
        add_kernel, "add", (1,), [whole(parts.shape)], [whole(shape)],
        [jax.ShapeDtypeStruct(shape, LOW)], [], 1 << 33, (jnp.zeros((1,), jnp.int32), parts), 1 << 24,
    )[0]


def place_of(distance):
    return bit("dp", distance).astype(jnp.int32).reshape(1)


def join_kernel(at_ref, first, second, both):
    b = at_ref[0]
    both[pl.ds(b, 1)] = first[...][None]
    both[pl.ds(1 - b, 1)] = second[...][None]


def join(first, second, distance):
    rows, columns = first.shape
    shape = (2, rows, columns)
    return call(
        join_kernel, "join", (1,), [whole(first.shape)] * 2, [whole(shape)],
        [jax.ShapeDtypeStruct(shape, LOW)], [], 1024, (place_of(distance), first, second), 1024,
    )[0].reshape(2 * rows, columns)


def settle_kernel(plan, size, at_ref, *refs):
    count = len(plan)
    outs = refs[2 * count :]
    depth = size.bit_length() - 1
    b = at_ref[0]
    for p, moves in enumerate(plan):
        rows = 2 * refs[2 * p].shape[0] // size
        for h in range(2):
            value = jnp.where(b == h, refs[2 * p][...], refs[2 * p + 1][...]).astype(FULL)
            for k in range(h, size, 2):
                at = sum(((k >> j) & 1) << (depth - 1 - j) for j in range(1, depth)) * rows
                for top, left, down, wide, out, to_row, to_column in moves:
                    low, high = max(top, k * rows), min(top + down, (k + 1) * rows)
                    if low < high:
                        start = to_row + low - top
                        source = at + low - k * rows
                        outs[out][start : start + high - low, to_column : to_column + wide] = value[
                            source : source + high - low, left : left + wide
                        ]


def settle(pairs, plan, shapes):
    args = [array for pair in pairs for array in pair]
    return call(
        partial(settle_kernel, plan, lax.axis_size("dp")),
        "settle",
        (1,),
        [whole(a.shape) for a in args],
        [whole(shape) for shape in shapes],
        [jax.ShapeDtypeStruct(shape, FULL) for shape in shapes],
        [],
        1024,
        (place_of(1), *args),
        1024,
    )


def shards(
    hidden_in,
    time_table,
    time_step,
    token_pos,
    heads_weight,
    merge_weight,
    lift_weight,
    lift_bias,
    drop_weight,
    drop_bias,
    modulate_weight,
    modulate_bias,
    first_gain,
    second_gain,
    out_grad,
):
    count = lax.axis_size("seq")
    place = lax.axis_index("seq")
    seqs, span, width = hidden_in.shape
    assert count == 4 and seqs == count
    length = span * count
    head = width // HEADS
    bits = powers(lax.axis_size("dp"))
    row_half = bit("dp", 1)
    me = jnp.stack([place, row_half]).astype(jnp.int32)

    units = drop_weight.shape[0]
    step = units // 2
    heads_pack = payload(blocks_of(heads_weight, width) + [merge_weight])
    heads_half = choose(heads_pack, row_half)
    heads_half, time_step = fence(heads_half, time_step)
    heads_across = swap(heads_half, "seq", 2)

    def feed_pack(h):
        columns = [lift_weight[:, j * units + h * step : j * units + (h + 1) * step] for j in range(4)]
        blocks = [jnp.concatenate(columns[k : k + 2], axis=1) for k in (0, 2)]
        return jnp.concatenate([drop_weight[h * step : (h + 1) * step]] + blocks, axis=0)

    table_rows, depth = time_table.shape
    chosen_rows = (time_step[:, None] == jnp.arange(table_rows, dtype=jnp.int32)[None, :]).astype(LOW)
    conds = jnp.dot(chosen_rows, time_table, preferred_element_type=FULL)
    modulation = matmul(conds.astype(LOW), modulate_weight, 1, 1) + modulate_bias.astype(FULL)
    columns = modulation.shape[1]
    vectors = [v.astype(FULL) for v in (lift_bias, drop_bias, first_gain, second_gain)]
    above = jnp.concatenate([modulation, token_pos.astype(FULL)], axis=1)
    below = jnp.concatenate(vectors)[None]
    below = jnp.pad(below, ((0, 0), (0, above.shape[1] - below.shape[1])))
    small = jnp.concatenate([above, below], axis=0)
    small_across = swap(small, "seq", 2)
    hidden_in, small = fence(hidden_in, small)
    heads_across, small, lift_weight, drop_weight = fence(
        heads_across, small, lift_weight, drop_weight
    )
    heads_handed = swap(heads_across, "dp", 1)
    heads_core = swap(heads_pack, "seq", 1), swap(heads_across, "seq", 1)
    hidden = lax.all_to_all(hidden_in, "seq", 0, 0, tiled=True).reshape(length, width)
    small = jnp.stack([small, small_across])
    small_core = swap(small, "seq", 1)
    small = jnp.stack([small[0], small_core[0], small[1], small_core[1]])
    small = choose_all(small, place)
    mine = lax.dynamic_index_in_dim(small, place, 1, keepdims=False)
    chosen = mine[:, :columns].reshape(6, width)
    positions = mine[:, columns:].reshape(length)
    rest = small[:, seqs]
    sizes = (lift_bias.shape[0], drop_bias.shape[0], first_gain.shape[0], second_gain.shape[0])
    vectors, at = [], 0
    for size in sizes:
        vectors.append(rest[:, at : at + size].reshape(1, -1))
        at += size
    up_bias, down_bias, gain_one, gain_two = vectors
    shift_a, scale_a, gate_a, shift_b, scale_b, gate_b = [chosen[k : k + 1] for k in range(6)]
    grow_a, grow_b = 1.0 + scale_a, 1.0 + scale_b

    def rows(*items):
        blank = jnp.zeros((8 - len(items), width), FULL)
        return jnp.concatenate(items + (blank,), axis=0)

    freqs = 10000.0 ** (-jnp.arange(0, head, 2, dtype=FULL) / head)
    freqs = jnp.tile(freqs, 2 * LANES // head)
    angles = positions[:, None] * freqs
    cosine, sine = jnp.cos(angles), jnp.sin(angles)

    pack_0, pack_1 = feed_pack(0), feed_pack(1)
    project_vectors = rows(gain_one, grow_a, shift_a)
    heads_handed, project_vectors, cosine, sine, pack_0, pack_1, me = fence(
        heads_handed, project_vectors, cosine, sine, pack_0, pack_1, me
    )
    heads = (
        heads_pack,
        heads_core[0],
        heads_across,
        heads_handed,
        heads_core[1],
        swap(heads_handed, "seq", 1),
    )
    hidden, heads, cosine, sine, pack_0, pack_1, out_grad = fence(
        hidden, heads, cosine, sine, pack_0, pack_1, out_grad
    )
    across_0 = swap(pack_0, "seq", 2)
    core_0, core_1 = swap(pack_0, "seq", 1), swap(pack_1, "seq", 1)
    adapted_a, query, key, value = project(
        me, hidden, project_vectors, heads, cosine, sine, head
    )
    merge_vectors, unmerge_vectors = rows(gate_a, gain_two, grow_b, shift_b), rows(gate_a, gain_two, grow_b)
    feed_vectors = rows(gate_b, down_bias)
    bias_0, bias_1 = [up_bias.reshape(4, 2, step)[:, h].reshape(1, 4 * step) for h in range(2)]
    query, merge_vectors, unmerge_vectors, feed_vectors, bias_0, bias_1 = fence(
        query, merge_vectors, unmerge_vectors, feed_vectors, bias_0, bias_1
    )
    query, out_grad = fence(query, out_grad)
    upstream = lax.all_to_all(out_grad, "seq", 0, 0, tiled=True).reshape(length, width)
    mixed, logsum = attend(me, query, key, value, head)
    mixed, logsum, across_0 = fence(mixed, logsum, across_0)
    mixed, pack_1 = fence(mixed, pack_1)
    other_0 = swap(across_0, "seq", 1)
    across_1 = swap(pack_1, "seq", 2)
    middle, adapted_b = merge(me, mixed, hidden, merge_vectors, heads)
    middle, adapted_b, core_0, other_0, upstream = fence(
        middle, adapted_b, core_0, other_0, upstream
    )
    pairs = width // LANES // 2
    adapted_b, upstream, core_1 = fence(adapted_b, upstream, core_1)
    lowered, grad, liftbias_0, keep_0, send_0 = feed(
        me, adapted_b, upstream, feed_vectors, bias_0, (pack_0, core_0, across_0, other_0)
    )
    lowered, grad, liftbias_0, keep_0, send_0, across_1 = fence(
        lowered, grad, liftbias_0, keep_0, send_0, across_1
    )
    other_1 = swap(across_1, "seq", 1)
    got_0 = swap(send_0, "seq", 1)
    *out_parts, adapted_b_grad, feed_sums, liftbias_1, keep_1, send_1 = feed(
        me, adapted_b, upstream, feed_vectors, bias_1, (pack_1, core_1, across_1, other_1),
        (lowered, grad, middle),
    )
    back = bits[::-1]
    last = len(back) - 1
    out_parts, adapted_b_grad, feed_sums, liftbias_1, keep_1, send_1, got_0 = fence(
        out_parts, adapted_b_grad, feed_sums, liftbias_1, keep_1, send_1, got_0
    )
    got_1 = swap(send_1, "seq", 1)
    core_0 = got_0
    adapted_b_grad, other_0 = fence(adapted_b_grad, sum_other(keep_0, core_0))
    got_0 = swap(other_0, "seq", 2)
    middle_grad, mixed_grad, merge_sums, merge_keep, merge_send = unmerge(
        me, adapted_b_grad, middle, upstream, mixed, unmerge_vectors, heads
    )
    middle_grad, mixed_grad, merge_sums, merge_keep, merge_send, got_1 = fence(
        middle_grad, mixed_grad, merge_sums, merge_keep, merge_send, got_1
    )
    heads_0, mine_1, other_1 = unattend(
        me, query, key, value, mixed, mixed_grad, logsum, cosine, sine, head, 0, pairs, (keep_1, got_1)
    )
    heads_0, mine_1, other_1, got_0 = fence(heads_0, mine_1, other_1, got_0)
    got_1 = swap(other_1, "seq", 2)
    heads_0, term_0 = fence(heads_0, sum_three(keep_0, core_0, got_0))
    parts_0 = deal(term_0)
    keep_2, send_2 = weigh(me, adapted_a, heads_0, (merge_keep, merge_send))
    mixed_grad, keep_2, send_2 = fence(mixed_grad, keep_2, send_2)
    got_2 = swap(send_2, "seq", 1)
    (heads_1,) = unattend(
        me, query, key, value, mixed, mixed_grad, logsum, cosine, sine, head, pairs, pairs
    )
    heads_1, got_1 = fence(heads_1, got_1)
    heads_1, term_1, parts_0 = fence(heads_1, sum_two(mine_1, got_1), parts_0)
    parts_1 = deal(term_1)
    heads_1, got_2 = fence(heads_1, got_2)
    keep_3, send_3, mine_2, other_2 = weigh(me, adapted_a, heads_1, (), (keep_2, got_2))
    keep_3, send_3, mine_2, other_2, parts_0 = fence(keep_3, send_3, mine_2, other_2, parts_0)
    got_3 = swap(send_3, "seq", 1)
    got_2 = swap(other_2, "seq", 2)
    term_0, core_3 = fence(add_up(parts_0), got_3)
    heads_1, term_0, other_3 = fence(heads_1, term_0, sum_other(keep_3, core_3))
    got_3 = swap(other_3, "seq", 2)
    got_0 = swap(term_0, "dp", back[0])
    *input_parts, project_sums = unproject(
        me, (heads_0, heads_1), hidden, middle_grad, rows(gain_one, grow_a), heads
    )
    input_parts, project_sums, got_0 = fence(input_parts, project_sums, got_0)
    input_parts, project_sums, term_0 = fence(
        input_parts, project_sums, join(term_0, got_0, back[0])
    )
    got_0 = swap(term_0, "dp", back[1])
    input_parts, project_sums, got_2, got_3, parts_1 = fence(
        input_parts, project_sums, got_2, got_3, parts_1
    )
    (mine_a, other_a), input_parts, project_sums, parts_1 = fence(
        split_beside((mine_2, got_2), (keep_3, core_3, got_3)), input_parts, project_sums, parts_1
    )
    got_a = swap(other_a, "dp", 1)
    liftbias_grad = jnp.stack([liftbias_0.reshape(4, step), liftbias_1.reshape(4, step)], axis=1)
    modulation_grad = jnp.concatenate(
        [project_sums[0:2], merge_sums[3:4], merge_sums[0:2], feed_sums[0:1]], axis=0
    ).reshape(count, columns)
    small = jnp.concatenate(
        [
            modulation_grad,
            liftbias_grad.reshape(count, -1),
            feed_sums[1].reshape(count, -1),
            project_sums[2].reshape(count, -1),
            merge_sums[2].reshape(count, -1),
        ],
        axis=1,
    )
    parts = [choose(small, place ^ d) for d in range(4)]
    term_1, parts = fence(add_up(parts_1), parts)
    got_1 = swap(term_1, "dp", back[0])
    parts = [swap(part, "seq", d) if d else part for d, part in enumerate(parts)]
    term_0, input_parts, parts = fence(join(term_0, got_0, back[1]), input_parts, parts)
    for k in range(2, last):
        term_0 = join(term_0, swap(term_0, "dp", back[k]), back[k])
    got_0 = swap(term_0, "dp", back[-1])
    input_parts = [swap(part, "seq", d) if d else part for d, part in enumerate(input_parts)]
    mine_a, got_a = fence(mine_a, got_a)
    mine_a, got_a, got_1, parts, term_0 = fence(mine_a, got_a, got_1, parts, term_0)
    term_a, got_1, parts, out_parts = fence(sum_two(mine_a, got_a), got_1, parts, out_parts)
    parts_a = deal(term_a, lax.axis_size("dp") // 2)
    term_1 = join(term_1, got_1, back[0])
    got_1 = swap(term_1, "dp", back[1])
    out_parts = [swap(part, "seq", d) if d else part for d, part in enumerate(out_parts)]
    small = choose_all(jnp.stack(parts), place)
    exact = lax.Precision.HIGHEST
    conds_grad = jnp.einsum(
        "sm,mc->sc", small[:, :columns], modulate_weight.astype(FULL), precision=exact
    )
    conds_grad = sum([swap(conds_grad, "seq", d) for d in (1, 2, 3)], conds_grad)
    spare = term_a.shape[1] // 2 - columns - 2 * depth
    above = jnp.concatenate(
        [
            small[:, :columns],
            conds,
            conds_grad,
            jnp.broadcast_to(time_step.astype(FULL)[:, None], (seqs, spare)),
        ],
        axis=1,
    )
    below = jnp.sum(small[:, columns:], axis=0)[None]
    below = jnp.pad(below, ((0, 7 - seqs), (0, above.shape[1] - below.shape[1])))
    small = jnp.concatenate([above, below], axis=0)
    upper = lax.reduce_precision(small, 8, 7)
    small = jnp.concatenate([upper, small - upper], axis=1).astype(LOW)
    small, parts_a = fence(small, parts_a)
    small, parts_a, got_1, input_parts = fence(small, parts_a, got_1, input_parts)
    term_a, got_1, input_parts = fence(gather_terms(small, parts_a), got_1, input_parts)
    parts_a = exchange(term_a)
    term_1 = join(term_1, got_1, back[1])
    for k in range(2, last):
        term_1 = join(term_1, swap(term_1, "dp", back[k]), back[k])
    got_1 = swap(term_1, "dp", back[-1])
    input_grad = lay(me, input_parts)
    parts_a, got_0 = fence(parts_a, got_0)
    parts_a, got_0, got_1, out_parts, input_grad = fence(
        parts_a, got_0, got_1, out_parts, input_grad
    )
    got_a = swap(parts_a, "dp", 1)
    block_out = lay(me, out_parts)
    pair_0, pair_1 = (term_0, got_0), (term_1, got_1)
    deep = width // 4
    drop_grad, lift_grad = settle(
        [pair_0, pair_1],
        [
            [(0, 0, step, width, 0, h * step, 0)]
            + [
                (step + (j >> 1) * deep, (j & 1) * step, deep, step, 1, 0, j * units + h * step)
                for j in range(4)
            ]
            for h in range(2)
        ],
        [drop_weight.shape, lift_weight.shape],
    )
    block_out, input_grad, drop_grad, lift_grad, parts_a, got_a = fence(
        block_out, input_grad, drop_grad, lift_grad, parts_a, got_a
    )
    share = table_rows // count
    (
        heads_grad, merge_grad, modulate_grad, modulatebias_grad,
        liftbias_out, dropbias_out, firstgain_out, secondgain_out, table_grad,
    ) = finish(me, parts_a, got_a, width, columns, depth, sizes, share)
    return (
        block_out,
        input_grad,
        heads_grad,
        merge_grad,
        lift_grad,
        liftbias_out,
        drop_grad,
        dropbias_out,
        modulate_grad,
        modulatebias_grad,
        firstgain_out,
        secondgain_out,
        table_grad,
    )


def solution(mesh):
    return jax.shard_map(
        shards,
        mesh=mesh,
        in_specs=(
            P("dp", "seq", None),
            P(),
            P("dp"),
            P("dp", "seq"),
            P("seq", None),
            P("seq", None),
            P("seq", None),
            P("seq"),
            P("seq", None),
            P("seq"),
            P("seq", None),
            P("seq"),
            P("seq"),
            P("seq"),
            P("dp", "seq", None),
        ),
        out_specs=(
            P("dp", "seq", None),
            P("dp", "seq", None),
            P("seq", None),
            P("seq", None),
            P("seq", None),
            P("seq"),
            P("seq", None),
            P("seq"),
            P("seq", None),
            P("seq"),
            P("seq"),
            P("seq"),
            P("seq", None),
        ),
        check_vma=False,
    )
```

profile of v0, /device:TPU:8, one launch (start us, length us, event | category | flops | bytes accessed | tf_op | source)
XLA Modules:
  0.0 376.7 jit_solution(5870398979247086580)
XLA Ops:
  5.8 3.6 all-to-all-start
  10.3 9.3 %collective-permute-done.p2 = bf16[384,768]{1,0:T(8,128)(2,1)} collective-permute-done((bf16[384,768]{1,0:T(8,128)(2,1)}, bf16[384,768]{1,0:T(8,128)(2,1)}, u32[]{:S(2)}, u32[]{:S(2)}) %collective-permute-start) | collective-permute-done | bytes 589856 | tf_op jit(solution)/shard_map/ppermute | solution.py:717
  23.2 5.5 %maximum_maximum_fusion = (bf16[768,768]{1,0:T(8,128)(2,1)}, bf16[768,768]{1,0:T(8,128)(2,1)}) fusion(bf16[192,384]{1,0:T(8,128)(2,1)S(1)} %get-tuple-element.513, bf16[192,384]{1,0:T(8,128)(2,1)S(1)} %get-tuple-element.514, bf16[192,384]{1,0:T(8,128)(2,1)S(1)} %get-tuple-element.515, bf16[192,384]{1,0:T(8,128)(2,1)S(1)} %get-tuple-element.516, ...), kind=kLoop, calls=%fused_computation.2 | loop fusion | flops 11796480 | bytes 4718592 | tf_op jit(solution)/shard_map/concatenate | solution.py:957
  30.0 3.1 multiply_sine_fusion
  34.4 2.5 all-to-all-done
  40.3 9.4 %project.1 = (bf16[768,1024]{1,0:T(8,128)(2,1)}, bf16[1024,768]{1,0:T(8,128)(2,1)}, bf16[1024,768]{1,0:T(8,128)(2,1)}, bf16[1024,768]{1,0:T(8,128)(2,1)}) custom-call(s32[2]{0:T(128)} %pad_add_fusion.me_ref.at_ref, bf16[1024,768]{1,0:T(8,128)(2,1)} %bitcast.48, f32[8,768]{1,0:T(8,128)} %get-tuple-element.273.vectors, bf16[2,384,768]{2,1,0:T(8,128)(2,1)} %copy-done.1, ...), custom_call_target="tpu_custom_call" | custom-call | flops 1024 | bytes 1024 | tf_op jit(solution)/shard_map/project/pallas_call | solution.py:25
  49.7 3.8 %all-to-all-start.1 = ((bf16[4,256,768]{2,1,0:T(8,128)(2,1)}), bf16[4,256,768]{2,1,0:T(8,128)(2,1)S(1)}, u32[]{:S(2)}, u32[]{:S(2)}) async-start(bf16[4,256,768]{2,1,0:T(8,128)(2,1)} %param.29), calls=%async_computation.1 | async-start | bytes 3145728 | tf_op jit(solution)/shard_map/all_to_all | solution.py:1031
  53.5 22.5 %attend.1 = (bf16[1024,768]{1,0:T(8,128)(2,1)}, f32[6,2,1024]{2,1,0:T(2,128)}) custom-call(s32[2]{0:T(128)} %pad_add_fusion.me_ref.at_ref, bf16[1024,768]{1,0:T(8,128)(2,1)} %get-tuple-element.286.query, bf16[1024,768]{1,0:T(8,128)(2,1)} %get-tuple-element.287.key, bf16[1024,768]{1,0:T(8,128)(2,1)} %get-tuple-element.288.value), custom_call_target="tpu_custom_call" | custom-call | flops 1024 | bytes 1024 | tf_op jit(solution)/shard_map/attend/pallas_call | solution.py:25
  76.6 1.9 collective-permute-start.11
  78.5 6.3 %merge.1 = (f32[1024,768]{1,0:T(8,128)}, bf16[1024,768]{1,0:T(8,128)(2,1)}) custom-call(s32[2]{0:T(128)} %pad_add_fusion.me_ref.at_ref, bf16[1024,768]{1,0:T(8,128)(2,1)} %get-tuple-element.294.mixed, bf16[1024,768]{1,0:T(8,128)(2,1)} %bitcast.49, f32[8,768]{1,0:T(8,128)} %concatenate.73.vectors, bf16[2,384,768]{2,1,0:T(8,128)(2,1)} %copy-done.1, ...), custom_call_target="tpu_custom_call" | custom-call | flops 1024 | bytes 1024 | tf_op jit(solution)/shard_map/merge/pallas_call | solution.py:25
  86.0 32.9 %feed.2 = (f32[1024,768]{1,0:T(8,128)}, f32[1024,768]{1,0:T(8,128)}, f32[1,1536]{1,0:T(1,128)}, bf16[2,768,768]{2,1,0:T(8,128)(2,1)}, bf16[2,768,768]{2,1,0:T(8,128)(2,1)}) custom-call(s32[2]{0:T(128)} %pad_add_fusion.me_ref.at_ref, bf16[1024,768]{1,0:T(8,128)(2,1)} %get-tuple-element.302.adapted, bf16[1024,768]{1,0:T(8,128)(2,1)} %bitcast.51, ...), custom_call_target="tpu_custom_call" | custom-call | flops 14495514624 | bytes 28311552 | tf_op jit(solution)/shard_map/feed/pallas_call | solution.py:25
  119.6 2.5 collective-permute-done.12.p3
  123.1 28.1 %feed.3 = (bf16[256,768]{1,0:T(8,128)(2,1)}, bf16[256,768]{1,0:T(8,128)(2,1)}, bf16[256,768]{1,0:T(8,128)(2,1)}, bf16[256,768]{1,0:T(8,128)(2,1)}, f32[1024,768]...) custom-call(s32[2]{0:T(128)} %pad_add_fusion.me_ref.at_ref, ...), custom_call_target="tpu_custom_call" | custom-call | flops 14495514624 | bytes 28311552 | tf_op jit(solution)/shard_map/feed/pallas_call | solution.py:25
  152.6 3.7 other.2
  156.4 11.4 %unmerge.1 = (f32[1024,768]{1,0:T(8,128)}, bf16[1024,768]{1,0:T(8,128)(2,1)}, f32[8,768]{1,0:T(8,128)}, bf16[2,192,768]{2,1,0:T(8,128)(2,1)}, bf16[2,192,768]{2,1,0:T(8,128)(2,1)}) custom-call(s32[2]{0:T(128)} %pad_add_fusion.me_ref.at_ref, f32[1024,768]{1,0:T(8,128)} %get-tuple-element.333.adapted_grad, f32[1024,768]{1,0:T(8,128)} %get-tuple-element.319.refs_2_.middle, ...), custom_call_target="tpu_custom_call" | custom-call | flops 1024 | bytes 1024 | tf_op jit(solution)/shard_map/unmerge/pallas_call | solution.py:25
  167.8 21.6 %unattend.2 = (bf16[3,1024,384]{2,1,0:T(8,128)(2,1)}, bf16[768,768]{1,0:T(8,128)(2,1)}, bf16[768,768]{1,0:T(8,128)(2,1)}) custom-call(s32[2]{0:T(128)} %pad_add_fusion.me_ref.at_ref, bf16[1024,768]{1,0:T(8,128)(2,1)} %get-tuple-element.286.query, bf16[1024,768]{1,0:T(8,128)(2,1)} %get-tuple-element.287.key, bf16[1024,768]{1,0:T(8,128)(2,1)} %get-tuple-element.288.value, ...), custom_call_target="tpu_custom_call" | custom-call | flops 1024 | bytes 1024 | tf_op jit(solution)/shard_map/unattend/pallas_call | solution.py:25
  190.4 3.0 two.3
  193.5 6.5 %all-to-all-start.2 = ((bf16[8,96,768]{2,1,0:T(8,128)(2,1)}), bf16[8,96,768]{2,1,0:T(8,128)(2,1)S(1)}, u32[]{:S(2)}, u32[]{:S(2)}) async-start(bf16[8,96,768]{2,1,0:T(8,128)(2,1)} %bitcast.64), calls=%async_computation.2 | async-start | bytes 2359296 | tf_op jit(solution)/shard_map/all_to_all | solution.py:843
  200.0 2.0 collective-permute-start.16
  201.9 6.5 %weigh.2 = (bf16[2,192,1920]{2,1,0:T(8,128)(2,1)}, bf16[2,192,1920]{2,1,0:T(8,128)(2,1)}) custom-call(s32[2]{0:T(128)} %pad_add_fusion.me_ref.at_ref, bf16[768,1024]{1,0:T(8,128)(2,1)} %get-tuple-element.282.turned, bf16[3,1024,384]{2,1,0:T(8,128)(2,1)} %get-tuple-element.351.grads.g0, bf16[2,192,768]{2,1,0:T(8,128)(2,1)} %get-tuple-element.352.refs_0_, ...), custom_call_target="tpu_custom_call" | custom-call | flops 1024 | bytes 1024 | tf_op jit(solution)/shard_map/weigh/pallas_call | solution.py:25
  208.6 20.0 %unattend.3.grads.g1 = bf16[3,1024,384]{2,1,0:T(8,128)(2,1)} custom-call(s32[2]{0:T(128)} %pad_add_fusion.me_ref.at_ref, bf16[1024,768]{1,0:T(8,128)(2,1)} %get-tuple-element.286.query, bf16[1024,768]{1,0:T(8,128)(2,1)} %get-tuple-element.287.key, bf16[1024,768]{1,0:T(8,128)(2,1)} %get-tuple-element.288.value, bf16[1024,768]{1,0:T(8,128)(2,1)} %get-tuple-element.294.mixed, ...), custom_call_target="tpu_custom_call" | custom-call | flops 1024 | bytes 1024 | tf_op jit(solution)/shard_map/unattend/pallas_call | solution.py:25
  228.5 2.6 two.4
  232.2 6.2 %all-to-all-start.3 = ((bf16[8,96,768]{2,1,0:T(8,128)(2,1)}), bf16[8,96,768]{2,1,0:T(8,128)(2,1)S(1)}, u32[]{:S(2)}, u32[]{:S(2)}) async-start(bf16[8,96,768]{2,1,0:T(8,128)(2,1)} %bitcast.63), calls=%async_computation.3 | async-start | bytes 2359296 | tf_op jit(solution)/shard_map/all_to_all | solution.py:843
  239.5 7.4 %weigh.3 = (bf16[2,192,1152]{2,1,0:T(8,128)(2,1)}, bf16[2,192,1152]{2,1,0:T(8,128)(2,1)}, bf16[192,1920]{1,0:T(8,128)(2,1)}, bf16[192,1920]{1,0:T(8,128)(2,1)}) custom-call(s32[2]{0:T(128)} %pad_add_fusion.me_ref.at_ref, bf16[768,1024]{1,0:T(8,128)(2,1)} %get-tuple-element.282.turned, bf16[3,1024,384]{2,1,0:T(8,128)(2,1)} %unattend.3.grads.g1, ...), custom_call_target="tpu_custom_call" | custom-call | flops 1024 | bytes 1024 | tf_op jit(solution)/shard_map/weigh/pallas_call | solution.py:25
  248.0 2.1 add.110.first
  251.0 2.0 other.3
  255.2 2.4 collective-permute-start.19
  257.7 12.3 %unproject.1 = (bf16[256,768]{1,0:T(8,128)(2,1)}, bf16[256,768]{1,0:T(8,128)(2,1)}, bf16[256,768]{1,0:T(8,128)(2,1)}, bf16[256,768]{1,0:T(8,128)(2,1)}, f32[8,768]{1,0:T(8,128)}) custom-call(s32[2]{0:T(128)} %pad_add_fusion.me_ref.at_ref, bf16[3,1024,384]{2,1,0:T(8,128)(2,1)} %get-tuple-element.351.grads.g0, bf16[3,1024,384]{2,1,0:T(8,128)(2,1)} %unattend.3.grads.g1, ...), custom_call_target="tpu_custom_call" | custom-call | flops 1024 | bytes 1024 | tf_op jit(solution)/shard_map/unproject/pallas_call | solution.py:25
  273.7 2.6 collective-permute-start.24
  277.1 2.9 beside.1
  281.4 2.1 add.111.first
  285.3 1.9 collective-permute-start.23
  289.0 1.9 join.5
  294.6 2.1 two.5
  296.9 5.1 %all-to-all-start.4 = ((bf16[4,24,3072]{2,1,0:T(8,128)(2,1)}), bf16[4,24,3072]{2,1,0:T(8,128)(2,1)S(1)}, u32[]{:S(2)}, u32[]{:S(2)}) async-start(bf16[4,24,3072]{2,1,0:T(8,128)(2,1)} %bitcast.70), calls=%async_computation.4 | async-start | bytes 1179648 | tf_op jit(solution)/shard_map/all_to_all | solution.py:843
  307.2 8.4 %all-to-all-done.4.parts = bf16[4,24,3072]{2,1,0:T(8,128)(2,1)S(1)} async-done(((bf16[4,24,3072]{2,1,0:T(8,128)(2,1)}), bf16[4,24,3072]{2,1,0:T(8,128)(2,1)S(1)}, u32[]{:S(2)}, u32[]{:S(2)}) %all-to-all-start.4) | async-done | bytes 589856 | tf_op jit(solution)/shard_map/all_to_all | solution.py:843
  315.6 1.8 collective-permute-done.34.refs_3_
  318.2 2.2 terms.1
  320.4 5.6 %all-to-all-start.5 = ((bf16[4,32,3072]{2,1,0:T(8,128)(2,1)}), bf16[4,32,3072]{2,1,0:T(8,128)(2,1)S(1)}, u32[]{:S(2)}, u32[]{:S(2)}) async-start(bf16[4,32,3072]{2,1,0:T(8,128)(2,1)} %terms.1), calls=%async_computation.5 | async-start | bytes 1572864 | tf_op jit(solution)/shard_map/all_to_all | solution.py:843
  327.3 1.9 join.7
  331.8 3.3 lay.2
  335.0 7.2 %collective-permute-done.35.refs_1_ = bf16[384,768]{1,0:T(8,128)(2,1)S(1)} collective-permute-done((bf16[384,768]{1,0:T(8,128)(2,1)S(1)}, bf16[384,768]{1,0:T(8,128)(2,1)S(1)}, u32[]{:S(2)}, u32[]{:S(2)}) %collective-permute-start.35) | collective-permute-done | bytes 589856 | tf_op jit(solution)/shard_map/ppermute | solution.py:717
  342.9 6.9 %collective-permute-done.39.refs_3_ = bf16[256,768]{1,0:T(8,128)(2,1)} collective-permute-done((bf16[256,768]{1,0:T(8,128)(2,1)}, bf16[256,768]{1,0:T(8,128)(2,1)}, u32[]{:S(2)}, u32[]{:S(2)}) %collective-permute-start.39) | collective-permute-done | bytes 393248 | tf_op jit(solution)/shard_map/ppermute | solution.py:717
  349.8 3.4 collective-permute-done.36.refs_3_
  354.5 4.0 %settle.1 = (f32[768,768]{1,0:T(8,128)}, f32[192,3072]{1,0:T(8,128)}) custom-call(s32[1]{0:T(128)} %bitcast.8.at_ref, bf16[384,768]{1,0:T(8,128)(2,1)} %bitcast.56, bf16[384,768]{1,0:T(8,128)(2,1)} %copy-done.15, bf16[384,768]{1,0:T(8,128)(2,1)} %bitcast.59, bf16[384,768]{1,0:T(8,128)(2,1)} %copy-done.16), custom_call_target="tpu_custom_call" | custom-call | flops 1024 | bytes 1024 | tf_op jit(solution)/shard_map/settle/pallas_call | solution.py:25
  358.5 3.3 lay.3
  361.8 9.3 %collective-permute-done.40.others = bf16[4,32,3072]{2,1,0:T(8,128)(2,1)S(1)} collective-permute-done((bf16[4,32,3072]{2,1,0:T(8,128)(2,1)S(1)}, bf16[4,32,3072]{2,1,0:T(8,128)(2,1)S(1)}, u32[]{:S(2)}, u32[]{:S(2)}) %collective-permute-start.40) | collective-permute-done | bytes 786464 | tf_op jit(solution)/shard_map/ppermute | solution.py:717
  372.0 4.5 %finish.1 = (f32[192,2304]{1,0:T(8,128)}, f32[192,768]{1,0:T(8,128)}, f32[1152,128]{1,0:T(8,128)}, f32[1152]{0:T(1024)}, f32[768]{0:T(1024)}, /*index=5*/f32[192...) custom-call(s32[2]{0:T(128)} %pad_add_fusion.me_ref.at_ref, bf16[4,32,3072]{2,1,0:T(8,128)(2,1)} %copy-done.5, ...), custom_call_target="tpu_custom_call" | custom-call | flops 1024 | bytes 1024 | tf_op jit(solution)/shard_map/finish/pallas_call | solution.py:25
  (234 shorter events, 53.7 us)
Async XLA Ops:
  2.1 34.7 %collective-permute-start.4 = (bf16[2,384,768]{2,1,0:T(8,128)(2,1)S(1)}, bf16[2,384,768]{2,1,0:T(8,128)(2,1)}, u32[]{:S(2)}, u32[]{:S(2)}) collective-permute-start(bf16[2,384,768]{2,1,0:T(8,128)(2,1)S(1)} %pad_maximum_fusion.p0), channel_id=1, source_target_pairs={{0,1},{1,0},{2,3},{3,2},{4,5},{5,4},{6,7},{7,6},{8,9},{9,8},{10,11... | collective-permute-start | bytes 3538952 | tf_op jit(solution)/shard_map/ppermute | solution.py:717
  3.1 16.4 %collective-permute-start = (bf16[384,768]{1,0:T(8,128)(2,1)}, bf16[384,768]{1,0:T(8,128)(2,1)}, u32[]{:S(2)}, u32[]{:S(2)}) collective-permute-start(bf16[384,768]{1,0:T(8,128)(2,1)} %dynamic-slice_bitcast_fusion), channel_id=1, source_target_pairs={{0,2},{1,3},{2,0},{3,1},{4,6},{5,7},{6,4},{7,5},{8,10},{9,11},{10,... | collective-permute-start | bytes 1769480 | tf_op jit(solution)/shard_map/ppermute | solution.py:717
  5.2 15.9 %collective-permute-start.2 = (f32[5,1408]{1,0:T(8,128)S(1)}, f32[5,1408]{1,0:T(8,128)S(1)}, u32[]{:S(2)}, u32[]{:S(2)}) collective-permute-start(f32[5,1408]{1,0:T(8,128)S(1)} %pad_maximum_fusion.5), channel_id=1, source_target_pairs={{0,2},{1,3},{2,0},{3,1},{4,6},{5,7},{6,4},{7,5},{8,10},{9,11},{10,... | collective-permute-start | bytes 84488 | tf_op jit(solution)/shard_map/ppermute | solution.py:717
  5.8 31.0 %all-to-all-start = ((bf16[4,256,768]{2,1,0:T(8,128)(2,1)}), bf16[4,256,768]{2,1,0:T(8,128)(2,1)S(1)}, u32[]{:S(2)}, u32[]{:S(2)}) async-start(bf16[4,256,768]{2,1,0:T(8,128)(2,1)} %param.15), calls=%async_computation | async-start | bytes 3145728 | tf_op jit(solution)/shard_map/all_to_all | solution.py:976
  19.5 14.8 %collective-permute-start.1 = (bf16[384,768]{1,0:T(8,128)(2,1)}, bf16[384,768]{1,0:T(8,128)(2,1)}, u32[]{:S(2)}, u32[]{:S(2)}) collective-permute-start(bf16[384,768]{1,0:T(8,128)(2,1)} %collective-permute-done.p2), channel_id=1, source_target_pairs={{0,4},{4,0},{8,12},{12,8},{16,20},{20,16},{24,28},{28,24},{1,5},{5... | collective-permute-start | bytes 1769480 | tf_op jit(solution)/shard_map/ppermute | solution.py:717
  21.1 15.8 %collective-permute-start.5 = (bf16[384,768]{1,0:T(8,128)(2,1)}, bf16[384,768]{1,0:T(8,128)(2,1)}, u32[]{:S(2)}, u32[]{:S(2)}) collective-permute-start(bf16[384,768]{1,0:T(8,128)(2,1)} %collective-permute-done.p2), channel_id=1, source_target_pairs={{0,1},{1,0},{2,3},{3,2},{4,5},{5,4},{6,7},{7,6},{8,9},{9,8},{10,11... | collective-permute-start | bytes 1769480 | tf_op jit(solution)/shard_map/ppermute | solution.py:717
  21.1 7.6 %collective-permute-start.3 = (f32[2,5,1408]{2,1,0:T(8,128)S(1)}, f32[2,5,1408]{2,1,0:T(8,128)S(1)}, u32[]{:S(2)}, u32[]{:S(2)}) collective-permute-start(f32[2,5,1408]{2,1,0:T(8,128)S(1)} %pad_maximum_fusion.3), channel_id=1, source_target_pairs={{0,1},{1,0},{2,3},{3,2},{4,5},{5,4},{6,7},{7,6},{8,9},{9,8},{10,11... | collective-permute-start | bytes 168968 | tf_op jit(solution)/shard_map/ppermute | solution.py:717
  34.3 2.5 collective-permute-start.6
  36.9 39.1 %collective-permute-start.7 = (bf16[768,768]{1,0:T(8,128)(2,1)}, bf16[768,768]{1,0:T(8,128)(2,1)}, u32[]{:S(2)}, u32[]{:S(2)}) collective-permute-start(bf16[768,768]{1,0:T(8,128)(2,1)} %get-tuple-element.291.p0), channel_id=1, source_target_pairs={{0,2},{1,3},{2,0},{3,1},{4,6},{5,7},{6,4},{7,5},{8,10},{9,11},{10,... | collective-permute-start | bytes 3538952 | tf_op jit(solution)/shard_map/ppermute | solution.py:717
  40.3 44.6 %collective-permute-start.8 = (bf16[768,768]{1,0:T(8,128)(2,1)}, bf16[768,768]{1,0:T(8,128)(2,1)}, u32[]{:S(2)}, u32[]{:S(2)}) collective-permute-start(bf16[768,768]{1,0:T(8,128)(2,1)} %get-tuple-element.291.p0), channel_id=1, source_target_pairs={{0,1},{1,0},{2,3},{3,2},{4,5},{5,4},{6,7},{7,6},{8,9},{9,8},{10,11... | collective-permute-start | bytes 3538952 | tf_op jit(solution)/shard_map/ppermute | solution.py:717
  49.7 35.2 %all-to-all-start.1 = ((bf16[4,256,768]{2,1,0:T(8,128)(2,1)}), bf16[4,256,768]{2,1,0:T(8,128)(2,1)S(1)}, u32[]{:S(2)}, u32[]{:S(2)}) async-start(bf16[4,256,768]{2,1,0:T(8,128)(2,1)} %param.29), calls=%async_computation.1 | async-start | bytes 3145728 | tf_op jit(solution)/shard_map/all_to_all | solution.py:1031
  53.5 23.0 %copy-start.13 = (bf16[768,768]{1,0:T(8,128)(2,1)S(1)}, bf16[768,768]{1,0:T(8,128)(2,1)}, u32[]{:S(2)}) copy-start(bf16[768,768]{1,0:T(8,128)(2,1)} %get-tuple-element.306.p0) | copy-start | bytes 3538948
  76.0 8.9 %collective-permute-start.9 = (bf16[768,768]{1,0:T(8,128)(2,1)}, bf16[768,768]{1,0:T(8,128)(2,1)}, u32[]{:S(2)}, u32[]{:S(2)}) collective-permute-start(bf16[768,768]{1,0:T(8,128)(2,1)} %collective-permute-done.7.p2), channel_id=1, source_target_pairs={{0,1},{1,0},{2,3},{3,2},{4,5},{5,4},{6,7},{7,6},{8,9},{9,8},{10,11... | collective-permute-start | bytes 3538952 | tf_op jit(solution)/shard_map/ppermute | solution.py:717
  76.5 8.4 %collective-permute-start.10 = (bf16[768,768]{1,0:T(8,128)(2,1)S(1)}, bf16[768,768]{1,0:T(8,128)(2,1)}, u32[]{:S(2)}, u32[]{:S(2)}) collective-permute-start(bf16[768,768]{1,0:T(8,128)(2,1)S(1)} %copy-done.13), channel_id=1, source_target_pairs={{0,1},{1,0},{2,3},{3,2},{4,5},{5,4},{6,7},{7,6},{8,9},{9,8},{10,11... | collective-permute-start | bytes 3538952 | tf_op jit(solution)/shard_map/ppermute | solution.py:717
  76.6 42.4 %collective-permute-start.11 = (bf16[768,768]{1,0:T(8,128)(2,1)S(1)}, bf16[768,768]{1,0:T(8,128)(2,1)}, u32[]{:S(2)}, u32[]{:S(2)}) collective-permute-start(bf16[768,768]{1,0:T(8,128)(2,1)S(1)} %copy-done.13), channel_id=1, source_target_pairs={{0,2},{1,3},{2,0},{3,1},{4,6},{5,7},{6,4},{7,5},{8,10},{9,11},{10,... | collective-permute-start | bytes 3538952 | tf_op jit(solution)/shard_map/ppermute | solution.py:717
  119.0 3.1 collective-permute-start.12
  119.1 32.1 %collective-permute-start.13 = (bf16[2,768,768]{2,1,0:T(8,128)(2,1)}, bf16[2,768,768]{2,1,0:T(8,128)(2,1)S(1)}, u32[]{:S(2)}, u32[]{:S(2)}) collective-permute-start(bf16[2,768,768]{2,1,0:T(8,128)(2,1)} %get-tuple-element.329), channel_id=1, source_target_pairs={{0,1},{1,0},{2,3},{3,2},{4,5},{5,4},{6,7},{7,6},{8,9},{9,8},{10,11... | collective-permute-start | bytes 7077896 | tf_op jit(solution)/shard_map/ppermute | solution.py:717
  151.2 16.6 %collective-permute-start.14 = (bf16[2,768,768]{2,1,0:T(8,128)(2,1)}, bf16[2,768,768]{2,1,0:T(8,128)(2,1)}, u32[]{:S(2)}, u32[]{:S(2)}) collective-permute-start(bf16[2,768,768]{2,1,0:T(8,128)(2,1)} %get-tuple-element.340), channel_id=1, source_target_pairs={{0,1},{1,0},{2,3},{3,2},{4,5},{5,4},{6,7},{7,6},{8,9},{9,8},{10,11... | collective-permute-start | bytes 7077896 | tf_op jit(solution)/shard_map/ppermute | solution.py:717
  156.3 33.1 %collective-permute-start.15 = (bf16[768,768]{1,0:T(8,128)(2,1)}, bf16[768,768]{1,0:T(8,128)(2,1)S(1)}, u32[]{:S(2)}, u32[]{:S(2)}) collective-permute-start(bf16[768,768]{1,0:T(8,128)(2,1)} %other.2), channel_id=1, source_target_pairs={{0,2},{1,3},{2,0},{3,1},{4,6},{5,7},{6,4},{7,5},{8,10},{9,11},{10,... | collective-permute-start | bytes 3538952 | tf_op jit(solution)/shard_map/ppermute | solution.py:717
  193.5 37.7 %all-to-all-start.2 = ((bf16[8,96,768]{2,1,0:T(8,128)(2,1)}), bf16[8,96,768]{2,1,0:T(8,128)(2,1)S(1)}, u32[]{:S(2)}, u32[]{:S(2)}) async-start(bf16[8,96,768]{2,1,0:T(8,128)(2,1)} %bitcast.64), calls=%async_computation.2 | async-start | bytes 2359296 | tf_op jit(solution)/shard_map/all_to_all | solution.py:843
  200.0 28.6 %collective-permute-start.16 = (bf16[768,768]{1,0:T(8,128)(2,1)}, bf16[768,768]{1,0:T(8,128)(2,1)}, u32[]{:S(2)}, u32[]{:S(2)}) collective-permute-start(bf16[768,768]{1,0:T(8,128)(2,1)} %get-tuple-element.357), channel_id=1, source_target_pairs={{0,2},{1,3},{2,0},{3,1},{4,6},{5,7},{6,4},{7,5},{8,10},{9,11},{10,... | collective-permute-start | bytes 3538952 | tf_op jit(solution)/shard_map/ppermute | solution.py:717
  208.5 29.9 %collective-permute-start.17 = (bf16[2,192,1920]{2,1,0:T(8,128)(2,1)}, bf16[2,192,1920]{2,1,0:T(8,128)(2,1)S(1)}, u32[]{:S(2)}, u32[]{:S(2)}) collective-permute-start(bf16[2,192,1920]{2,1,0:T(8,128)(2,1)} %get-tuple-element.363), channel_id=1, source_target_pairs={{0,1},{1,0},{2,3},{3,2},{4,5},{5,4},{6,7},{7,6},{8,9},{9,8},{10,11... | collective-permute-start | bytes 4423688 | tf_op jit(solution)/shard_map/ppermute | solution.py:717
  232.2 44.1 %all-to-all-start.3 = ((bf16[8,96,768]{2,1,0:T(8,128)(2,1)}), bf16[8,96,768]{2,1,0:T(8,128)(2,1)S(1)}, u32[]{:S(2)}, u32[]{:S(2)}) async-start(bf16[8,96,768]{2,1,0:T(8,128)(2,1)} %bitcast.63), calls=%async_computation.3 | async-start | bytes 2359296 | tf_op jit(solution)/shard_map/all_to_all | solution.py:843
  246.9 3.2 collective-permute-start.18
  247.1 29.2 %collective-permute-start.20 = (bf16[192,1920]{1,0:T(8,128)(2,1)}, bf16[192,1920]{1,0:T(8,128)(2,1)}, u32[]{:S(2)}, u32[]{:S(2)}) collective-permute-start(bf16[192,1920]{1,0:T(8,128)(2,1)} %get-tuple-element.397), channel_id=1, source_target_pairs={{0,2},{1,3},{2,0},{3,1},{4,6},{5,7},{6,4},{7,5},{8,10},{9,11},{10,... | collective-permute-start | bytes 2211848 | tf_op jit(solution)/shard_map/ppermute | solution.py:717
  253.0 23.2 %collective-permute-start.21 = (bf16[192,1152]{1,0:T(8,128)(2,1)}, bf16[192,1152]{1,0:T(8,128)(2,1)S(1)}, u32[]{:S(2)}, u32[]{:S(2)}) collective-permute-start(bf16[192,1152]{1,0:T(8,128)(2,1)} %other.3), channel_id=1, source_target_pairs={{0,2},{1,3},{2,0},{3,1},{4,6},{5,7},{6,4},{7,5},{8,10},{9,11},{10,... | collective-permute-start | bytes 1327112 | tf_op jit(solution)/shard_map/ppermute | solution.py:717
  255.2 16.1 %collective-permute-start.19 = (bf16[96,768]{1,0:T(8,128)(2,1)S(1)}, bf16[96,768]{1,0:T(8,128)(2,1)S(1)}, u32[]{:S(2)}, u32[]{:S(2)}) collective-permute-start(bf16[96,768]{1,0:T(8,128)(2,1)S(1)} %copy-done.26), channel_id=1, source_target_pairs={{0,16},{4,20},{8,24},{12,28},{16,0},{20,4},{24,8},{28,12},{1,17},{... | collective-permute-start | bytes 442376 | tf_op jit(solution)/shard_map/ppermute | solution.py:717
  273.7 14.3 %collective-permute-start.24 = (bf16[192,768]{1,0:T(8,128)(2,1)}, bf16[192,768]{1,0:T(8,128)(2,1)S(1)}, u32[]{:S(2)}, u32[]{:S(2)}) collective-permute-start(bf16[192,768]{1,0:T(8,128)(2,1)} %bitcast.65), channel_id=1, source_target_pairs={{0,8},{4,12},{8,0},{12,4},{16,24},{20,28},{24,16},{28,20},{1,9},{5... | collective-permute-start | bytes 884744 | tf_op jit(solution)/shard_map/ppermute | solution.py:717
  280.0 14.6 %collective-permute-start.22 = (bf16[96,3072]{1,0:T(8,128)(2,1)}, bf16[96,3072]{1,0:T(8,128)(2,1)}, u32[]{:S(2)}, u32[]{:S(2)}) collective-permute-start(bf16[96,3072]{1,0:T(8,128)(2,1)} %get-tuple-element.411), channel_id=1, source_target_pairs={{0,4},{4,0},{8,12},{12,8},{16,20},{20,16},{24,28},{28,24},{1,5},{5... | collective-permute-start | bytes 1769480 | tf_op jit(solution)/shard_map/ppermute | solution.py:717
  285.3 9.3 %collective-permute-start.23 = (bf16[96,768]{1,0:T(8,128)(2,1)}, bf16[96,768]{1,0:T(8,128)(2,1)S(1)}, u32[]{:S(2)}, u32[]{:S(2)}) collective-permute-start(bf16[96,768]{1,0:T(8,128)(2,1)} %add.111.first), channel_id=1, source_target_pairs={{0,16},{4,20},{8,24},{12,28},{16,0},{20,4},{24,8},{28,12},{1,17},{... | collective-permute-start | bytes 442376 | tf_op jit(solution)/shard_map/ppermute | solution.py:717
  287.2 3.8 %collective-permute-start.25 = (f32[2496]{0:T(1024)S(1)}, f32[2496]{0:T(1024)S(1)}, u32[]{:S(2)}, u32[]{:S(2)}) collective-permute-start(f32[2496]{0:T(1024)S(1)} %get-tuple-element.427), channel_id=1, source_target_pairs={{0,1},{1,0},{2,3},{3,2},{4,5},{5,4},{6,7},{7,6},{8,9},{9,8},{10,11... | collective-permute-start | bytes 29960 | tf_op jit(solution)/shard_map/ppermute | solution.py:717
  287.2 3.8 %collective-permute-start.26 = (f32[2496]{0:T(1024)S(1)}, f32[2496]{0:T(1024)S(1)}, u32[]{:S(2)}, u32[]{:S(2)}) collective-permute-start(f32[2496]{0:T(1024)S(1)} %get-tuple-element.428), channel_id=1, source_target_pairs={{0,2},{1,3},{2,0},{3,1},{4,6},{5,7},{6,4},{7,5},{8,10},{9,11},{10,... | collective-permute-start | bytes 29960 | tf_op jit(solution)/shard_map/ppermute | solution.py:717
  288.1 3.1 collective-permute-start.27
  291.2 24.4 %collective-permute-start.32 = (bf16[256,768]{1,0:T(8,128)(2,1)}, bf16[256,768]{1,0:T(8,128)(2,1)S(1)}, u32[]{:S(2)}, u32[]{:S(2)}) collective-permute-start(bf16[256,768]{1,0:T(8,128)(2,1)} %get-tuple-element.455), channel_id=1, source_target_pairs={{0,1},{1,0},{2,3},{3,2},{4,5},{5,4},{6,7},{7,6},{8,9},{9,8},{10,11... | collective-permute-start | bytes 1179656 | tf_op jit(solution)/shard_map/ppermute | solution.py:717
  291.8 23.8 %collective-permute-start.33 = (bf16[256,768]{1,0:T(8,128)(2,1)}, bf16[256,768]{1,0:T(8,128)(2,1)S(1)}, u32[]{:S(2)}, u32[]{:S(2)}) collective-permute-start(bf16[256,768]{1,0:T(8,128)(2,1)} %get-tuple-element.456), channel_id=1, source_target_pairs={{0,2},{1,3},{2,0},{3,1},{4,6},{5,7},{6,4},{7,5},{8,10},{9,11},{10,... | collective-permute-start | bytes 1179656 | tf_op jit(solution)/shard_map/ppermute | solution.py:717
  296.9 18.7 %all-to-all-start.4 = ((bf16[4,24,3072]{2,1,0:T(8,128)(2,1)}), bf16[4,24,3072]{2,1,0:T(8,128)(2,1)S(1)}, u32[]{:S(2)}, u32[]{:S(2)}) async-start(bf16[4,24,3072]{2,1,0:T(8,128)(2,1)} %bitcast.70), calls=%async_computation.4 | async-start | bytes 1179648 | tf_op jit(solution)/shard_map/all_to_all | solution.py:843
  302.2 3.7 collective-permute-start.30
  302.3 4.2 %collective-permute-start.29 = (f32[4,128]{1,0:T(4,128)S(1)}, f32[4,128]{1,0:T(4,128)S(1)}, u32[]{:S(2)}, u32[]{:S(2)}) collective-permute-start(f32[4,128]{1,0:T(4,128)S(1)} %fusion.13), channel_id=1, source_target_pairs={{0,2},{1,3},{2,0},{3,1},{4,6},{5,7},{6,4},{7,5},{8,10},{9,11},{10,... | collective-permute-start | bytes 6152 | tf_op jit(solution)/shard_map/ppermute | solution.py:717
  303.2 3.2 collective-permute-start.28
  305.9 11.5 %collective-permute-start.34 = (bf16[256,768]{1,0:T(8,128)(2,1)}, bf16[256,768]{1,0:T(8,128)(2,1)S(1)}, u32[]{:S(2)}, u32[]{:S(2)}) collective-permute-start(bf16[256,768]{1,0:T(8,128)(2,1)} %get-tuple-element.457), channel_id=1, source_target_pairs={{0,3},{1,2},{2,1},{3,0},{4,7},{5,6},{6,5},{7,4},{8,11},{9,10},{10,... | collective-permute-start | bytes 1179656 | tf_op jit(solution)/shard_map/ppermute | solution.py:717
  306.4 11.8 %collective-permute-start.31 = (bf16[192,768]{1,0:T(8,128)(2,1)}, bf16[192,768]{1,0:T(8,128)(2,1)S(1)}, u32[]{:S(2)}, u32[]{:S(2)}) collective-permute-start(bf16[192,768]{1,0:T(8,128)(2,1)} %bitcast.67), channel_id=1, source_target_pairs={{0,8},{4,12},{8,0},{12,4},{16,24},{20,28},{24,16},{28,20},{1,9},{5... | collective-permute-start | bytes 884744 | tf_op jit(solution)/shard_map/ppermute | solution.py:717
  320.4 22.5 %all-to-all-start.5 = ((bf16[4,32,3072]{2,1,0:T(8,128)(2,1)}), bf16[4,32,3072]{2,1,0:T(8,128)(2,1)S(1)}, u32[]{:S(2)}, u32[]{:S(2)}) async-start(bf16[4,32,3072]{2,1,0:T(8,128)(2,1)} %terms.1), calls=%async_computation.5 | async-start | bytes 1572864 | tf_op jit(solution)/shard_map/all_to_all | solution.py:843
  326.0 16.3 %collective-permute-start.35 = (bf16[384,768]{1,0:T(8,128)(2,1)S(1)}, bf16[384,768]{1,0:T(8,128)(2,1)S(1)}, u32[]{:S(2)}, u32[]{:S(2)}) collective-permute-start(bf16[384,768]{1,0:T(8,128)(2,1)S(1)} %bitcast.57), channel_id=1, source_target_pairs={{0,4},{4,0},{8,12},{12,8},{16,20},{20,16},{24,28},{28,24},{1,5},{5... | collective-permute-start | bytes 1769480 | tf_op jit(solution)/shard_map/ppermute | solution.py:717
  329.2 24.0 %collective-permute-start.36 = (bf16[384,768]{1,0:T(8,128)(2,1)}, bf16[384,768]{1,0:T(8,128)(2,1)S(1)}, u32[]{:S(2)}, u32[]{:S(2)}) collective-permute-start(bf16[384,768]{1,0:T(8,128)(2,1)} %bitcast.58), channel_id=1, source_target_pairs={{0,4},{4,0},{8,12},{12,8},{16,20},{20,16},{24,28},{28,24},{1,5},{5... | collective-permute-start | bytes 1769480 | tf_op jit(solution)/shard_map/ppermute | solution.py:717
  329.9 13.0 %collective-permute-start.37 = (bf16[256,768]{1,0:T(8,128)(2,1)}, bf16[256,768]{1,0:T(8,128)(2,1)S(1)}, u32[]{:S(2)}, u32[]{:S(2)}) collective-permute-start(bf16[256,768]{1,0:T(8,128)(2,1)} %get-tuple-element.470), channel_id=1, source_target_pairs={{0,1},{1,0},{2,3},{3,2},{4,5},{5,4},{6,7},{7,6},{8,9},{9,8},{10,11... | collective-permute-start | bytes 1179656 | tf_op jit(solution)/shard_map/ppermute | solution.py:717
  329.9 13.0 %collective-permute-start.38 = (bf16[256,768]{1,0:T(8,128)(2,1)}, bf16[256,768]{1,0:T(8,128)(2,1)}, u32[]{:S(2)}, u32[]{:S(2)}) collective-permute-start(bf16[256,768]{1,0:T(8,128)(2,1)} %get-tuple-element.471), channel_id=1, source_target_pairs={{0,2},{1,3},{2,0},{3,1},{4,6},{5,7},{6,4},{7,5},{8,10},{9,11},{10,... | collective-permute-start | bytes 1179656 | tf_op jit(solution)/shard_map/ppermute | solution.py:717
  330.9 18.9 %collective-permute-start.39 = (bf16[256,768]{1,0:T(8,128)(2,1)}, bf16[256,768]{1,0:T(8,128)(2,1)}, u32[]{:S(2)}, u32[]{:S(2)}) collective-permute-start(bf16[256,768]{1,0:T(8,128)(2,1)} %get-tuple-element.472), channel_id=1, source_target_pairs={{0,3},{1,2},{2,1},{3,0},{4,7},{5,6},{6,5},{7,4},{8,11},{9,10},{10,... | collective-permute-start | bytes 1179656 | tf_op jit(solution)/shard_map/ppermute | solution.py:717
  353.2 17.9 %collective-permute-start.40 = (bf16[4,32,3072]{2,1,0:T(8,128)(2,1)S(1)}, bf16[4,32,3072]{2,1,0:T(8,128)(2,1)S(1)}, u32[]{:S(2)}, u32[]{:S(2)}) collective-permute-start(bf16[4,32,3072]{2,1,0:T(8,128)(2,1)S(1)} %all-to-all-done.5.parts), channel_id=1, source_target_pairs={{0,4},{4,0},{8,12},{12,8},{16,20},{20,16},{24,28},{28,24},{1,5},{5... | collective-permute-start | bytes 2359304 | tf_op jit(solution)/shard_map/ppermute | solution.py:717
  (40 other events, 170.2 us)
where the time goes:
time: 382 us; the launch traced here: 377 us
  Pallas kernels  223 us (58%)
  starting transfers between devices  63.8 us (17%)
  waiting for transfers between devices  57.2 us (15%)
  local copies, waits for them, and re-layouts  19.1 us (5%)
  other arithmetic  11 us (3%)
    pallas_call x28, Pallas kernels, call(): pl.pallas_call(body, name=name, grid_spec=pltpu.PrefetchScalarGridSpec(nu...  223 us
    ppermute x41, waiting for transfers between devices, swap(): return lax.ppermute(array, axis, [(i, i ^ distance) for i in range(size)])  45.7 us
    ppermute x41, starting transfers between devices, swap(): return lax.ppermute(array, axis, [(i, i ^ distance) for i in range(size)])  32.9 us
    all_to_all x4, starting transfers between devices, exchange(): lax.all_to_all(parts, 'dp', 0, 0, axis_index_groups=groups, tiled=True)  23.4 us
    unnamed x88, local copies, waits for them, and re-layouts  11.1 us
    all_to_all x4, waiting for transfers between devices, exchange(): lax.all_to_all(parts, 'dp', 0, 0, axis_index_groups=groups, tiled=True)  9.05 us
  transfers between devices with their start and end apart: 47, of which 15 were waited for; matrix products, arithmetic and copies ran while one was open for 5% of the time, Pallas kernels for 57%

commit v1 on v0

--- a/solution.py
+++ b/solution.py
@@ -1128,12 +1128,14 @@
     term_0, input_parts, parts = fence(join(term_0, got_0, back[1]), input_parts, parts)
     for k in range(2, last):
         term_0 = join(term_0, swap(term_0, "dp", back[k]), back[k])
-    got_0 = swap(term_0, "dp", back[-1])
     input_parts = [swap(part, "seq", d) if d else part for d, part in enumerate(input_parts)]
     mine_a, got_a = fence(mine_a, got_a)
     mine_a, got_a, got_1, parts, term_0 = fence(mine_a, got_a, got_1, parts, term_0)
-    term_a, got_1, parts, out_parts = fence(sum_two(mine_a, got_a), got_1, parts, out_parts)
+    term_a, got_1, parts, out_parts, term_0 = fence(
+        sum_two(mine_a, got_a), got_1, parts, out_parts, term_0
+    )
     parts_a = deal(term_a, lax.axis_size("dp") // 2)
+    got_0 = swap(term_0, "dp", back[-1])
     term_1 = join(term_1, got_1, back[0])
     got_1 = swap(term_1, "dp", back[1])
     out_parts = [swap(part, "seq", d) if d else part for d, part in enumerate(out_parts)]
@@ -1159,6 +1161,7 @@
     upper = lax.reduce_precision(small, 8, 7)
     small = jnp.concatenate([upper, small - upper], axis=1).astype(LOW)
     small, parts_a = fence(small, parts_a)
+    small, parts_a, got_0 = fence(small, parts_a, got_0)
     small, parts_a, got_1, input_parts = fence(small, parts_a, got_1, input_parts)
     term_a, got_1, input_parts = fence(gather_terms(small, parts_a), got_1, input_parts)
     parts_a = exchange(term_a)
@@ -1167,10 +1170,7 @@
         term_1 = join(term_1, swap(term_1, "dp", back[k]), back[k])
     got_1 = swap(term_1, "dp", back[-1])
     input_grad = lay(me, input_parts)
-    parts_a, got_0 = fence(parts_a, got_0)
-    parts_a, got_0, got_1, out_parts, input_grad = fence(
-        parts_a, got_0, got_1, out_parts, input_grad
-    )
+    parts_a, got_1, input_grad = fence(parts_a, got_1, input_grad)
     got_a = swap(parts_a, "dp", 1)
     block_out = lay(me, out_parts)
     pair_0, pair_1 = (term_0, got_0), (term_1, got_1)

time: 382 us -> 390 us (1.021)
    ppermute x41, waiting for transfers between devices: 45.7 us -> 51.3 us  [swap(): return lax.ppermute(array, axis, [(i, i ^ distance) for i in range(size)])]
    unnamed x88 -> x94, local copies, waits for them, and re-layouts: 11.1 us -> 12.7 us
  transfers between devices with their start and end apart: 47 -> 47, of which waited for: 15 -> 14; matrix products, arithmetic and copies ran while one was open for 5% -> 5% of each run, Pallas kernels for 57% -> 56%
where the time goes in v1:
time: 390 us; the launch traced here: 382 us
  Pallas kernels  224 us (57%)
  starting transfers between devices  64.4 us (17%)
  waiting for transfers between devices  60.1 us (15%)
  local copies, waits for them, and re-layouts  20.7 us (5%)
  other arithmetic  10.9 us (3%)
    pallas_call x28, Pallas kernels, call(): pl.pallas_call(body, name=name, grid_spec=pltpu.PrefetchScalarGridSpec(nu...  224 us
    ppermute x41, waiting for transfers between devices, swap(): return lax.ppermute(array, axis, [(i, i ^ distance) for i in range(size)])  51.3 us
    ppermute x41, starting transfers between devices, swap(): return lax.ppermute(array, axis, [(i, i ^ distance) for i in range(size)])  34.1 us
    all_to_all x4, starting transfers between devices, exchange(): lax.all_to_all(parts, 'dp', 0, 0, axis_index_groups=groups, tiled=True)  22.9 us
    unnamed x94, local copies, waits for them, and re-layouts  12.7 us
  transfers between devices with their start and end apart: 47, of which 14 were waited for; matrix products, arithmetic and copies ran while one was open for 5% of the time, Pallas kernels for 56%

profile of v1, /device:TPU:8, one launch (start us, length us, event | category | flops | bytes accessed | tf_op | source)
XLA Modules:
  0.0 382.3 jit_solution(8495404735836317651)
XLA Ops:
  5.8 3.6 all-to-all-start
  10.3 9.2 %collective-permute-done.p2 = bf16[384,768]{1,0:T(8,128)(2,1)} collective-permute-done((bf16[384,768]{1,0:T(8,128)(2,1)}, bf16[384,768]{1,0:T(8,128)(2,1)}, u32[]{:S(2)}, u32[]{:S(2)}) %collective-permute-start) | collective-permute-done | bytes 589856 | tf_op jit(solution)/shard_map/ppermute | solution.py:717
  23.2 5.5 %maximum_maximum_fusion = (bf16[768,768]{1,0:T(8,128)(2,1)}, bf16[768,768]{1,0:T(8,128)(2,1)}) fusion(bf16[192,384]{1,0:T(8,128)(2,1)S(1)} %get-tuple-element.507, bf16[192,384]{1,0:T(8,128)(2,1)S(1)} %get-tuple-element.508, bf16[192,384]{1,0:T(8,128)(2,1)S(1)} %get-tuple-element.509, bf16[192,384]{1,0:T(8,128)(2,1)S(1)} %get-tuple-element.510, ...), kind=kLoop, calls=%fused_computation.2 | loop fusion | flops 11796480 | bytes 4718592 | tf_op jit(solution)/shard_map/concatenate | solution.py:957
  30.0 3.1 multiply_sine_fusion
  34.4 2.5 all-to-all-done
  40.3 9.4 %project.1 = (bf16[768,1024]{1,0:T(8,128)(2,1)}, bf16[1024,768]{1,0:T(8,128)(2,1)}, bf16[1024,768]{1,0:T(8,128)(2,1)}, bf16[1024,768]{1,0:T(8,128)(2,1)}) custom-call(s32[2]{0:T(128)} %pad_add_fusion.me_ref.at_ref, bf16[1024,768]{1,0:T(8,128)(2,1)} %bitcast.48, f32[8,768]{1,0:T(8,128)} %get-tuple-element.270.vectors, bf16[2,384,768]{2,1,0:T(8,128)(2,1)} %copy-done.1, ...), custom_call_target="tpu_custom_call" | custom-call | flops 1024 | bytes 1024 | tf_op jit(solution)/shard_map/project/pallas_call | solution.py:25
  49.7 3.8 %all-to-all-start.1 = ((bf16[4,256,768]{2,1,0:T(8,128)(2,1)}), bf16[4,256,768]{2,1,0:T(8,128)(2,1)S(1)}, u32[]{:S(2)}, u32[]{:S(2)}) async-start(bf16[4,256,768]{2,1,0:T(8,128)(2,1)} %param.29), calls=%async_computation.1 | async-start | bytes 3145728 | tf_op jit(solution)/shard_map/all_to_all | solution.py:1031
  53.5 22.5 %attend.1 = (bf16[1024,768]{1,0:T(8,128)(2,1)}, f32[6,2,1024]{2,1,0:T(2,128)}) custom-call(s32[2]{0:T(128)} %pad_add_fusion.me_ref.at_ref, bf16[1024,768]{1,0:T(8,128)(2,1)} %get-tuple-element.283.query, bf16[1024,768]{1,0:T(8,128)(2,1)} %get-tuple-element.284.key, bf16[1024,768]{1,0:T(8,128)(2,1)} %get-tuple-element.285.value), custom_call_target="tpu_custom_call" | custom-call | flops 1024 | bytes 1024 | tf_op jit(solution)/shard_map/attend/pallas_call | solution.py:25
  76.6 1.9 collective-permute-start.11
  78.6 6.4 %merge.1 = (f32[1024,768]{1,0:T(8,128)}, bf16[1024,768]{1,0:T(8,128)(2,1)}) custom-call(s32[2]{0:T(128)} %pad_add_fusion.me_ref.at_ref, bf16[1024,768]{1,0:T(8,128)(2,1)} %get-tuple-element.291.mixed, bf16[1024,768]{1,0:T(8,128)(2,1)} %bitcast.49, f32[8,768]{1,0:T(8,128)} %concatenate.73.vectors, bf16[2,384,768]{2,1,0:T(8,128)(2,1)} %copy-done.1, ...), custom_call_target="tpu_custom_call" | custom-call | flops 1024 | bytes 1024 | tf_op jit(solution)/shard_map/merge/pallas_call | solution.py:25
  86.1 32.9 %feed.2 = (f32[1024,768]{1,0:T(8,128)}, f32[1024,768]{1,0:T(8,128)}, f32[1,1536]{1,0:T(1,128)}, bf16[2,768,768]{2,1,0:T(8,128)(2,1)}, bf16[2,768,768]{2,1,0:T(8,128)(2,1)}) custom-call(s32[2]{0:T(128)} %pad_add_fusion.me_ref.at_ref, bf16[1024,768]{1,0:T(8,128)(2,1)} %get-tuple-element.299.adapted, bf16[1024,768]{1,0:T(8,128)(2,1)} %bitcast.51, ...), custom_call_target="tpu_custom_call" | custom-call | flops 14495514624 | bytes 28311552 | tf_op jit(solution)/shard_map/feed/pallas_call | solution.py:25
  119.6 2.5 collective-permute-done.12.p3
  123.1 28.0 %feed.3 = (bf16[256,768]{1,0:T(8,128)(2,1)}, bf16[256,768]{1,0:T(8,128)(2,1)}, bf16[256,768]{1,0:T(8,128)(2,1)}, bf16[256,768]{1,0:T(8,128)(2,1)}, f32[1024,768]...) custom-call(s32[2]{0:T(128)} %pad_add_fusion.me_ref.at_ref, ...), custom_call_target="tpu_custom_call" | custom-call | flops 14495514624 | bytes 28311552 | tf_op jit(solution)/shard_map/feed/pallas_call | solution.py:25
  152.6 3.7 other.2
  156.4 11.4 %unmerge.1 = (f32[1024,768]{1,0:T(8,128)}, bf16[1024,768]{1,0:T(8,128)(2,1)}, f32[8,768]{1,0:T(8,128)}, bf16[2,192,768]{2,1,0:T(8,128)(2,1)}, bf16[2,192,768]{2,1,0:T(8,128)(2,1)}) custom-call(s32[2]{0:T(128)} %pad_add_fusion.me_ref.at_ref, f32[1024,768]{1,0:T(8,128)} %get-tuple-element.330.adapted_grad, f32[1024,768]{1,0:T(8,128)} %get-tuple-element.316.refs_2_.middle, ...), custom_call_target="tpu_custom_call" | custom-call | flops 1024 | bytes 1024 | tf_op jit(solution)/shard_map/unmerge/pallas_call | solution.py:25
  167.8 21.6 %unattend.2 = (bf16[3,1024,384]{2,1,0:T(8,128)(2,1)}, bf16[768,768]{1,0:T(8,128)(2,1)}, bf16[768,768]{1,0:T(8,128)(2,1)}) custom-call(s32[2]{0:T(128)} %pad_add_fusion.me_ref.at_ref, bf16[1024,768]{1,0:T(8,128)(2,1)} %get-tuple-element.283.query, bf16[1024,768]{1,0:T(8,128)(2,1)} %get-tuple-element.284.key, bf16[1024,768]{1,0:T(8,128)(2,1)} %get-tuple-element.285.value, ...), custom_call_target="tpu_custom_call" | custom-call | flops 1024 | bytes 1024 | tf_op jit(solution)/shard_map/unattend/pallas_call | solution.py:25
  190.4 3.0 two.3
  193.4 6.5 %all-to-all-start.2 = ((bf16[8,96,768]{2,1,0:T(8,128)(2,1)}), bf16[8,96,768]{2,1,0:T(8,128)(2,1)S(1)}, u32[]{:S(2)}, u32[]{:S(2)}) async-start(bf16[8,96,768]{2,1,0:T(8,128)(2,1)} %bitcast.64), calls=%async_computation.2 | async-start | bytes 2359296 | tf_op jit(solution)/shard_map/all_to_all | solution.py:843
  199.9 2.0 collective-permute-start.16
  201.9 6.6 %weigh.2 = (bf16[2,192,1920]{2,1,0:T(8,128)(2,1)}, bf16[2,192,1920]{2,1,0:T(8,128)(2,1)}) custom-call(s32[2]{0:T(128)} %pad_add_fusion.me_ref.at_ref, bf16[768,1024]{1,0:T(8,128)(2,1)} %get-tuple-element.279.turned, bf16[3,1024,384]{2,1,0:T(8,128)(2,1)} %get-tuple-element.348.grads.g0, bf16[2,192,768]{2,1,0:T(8,128)(2,1)} %get-tuple-element.349.refs_0_, ...), custom_call_target="tpu_custom_call" | custom-call | flops 1024 | bytes 1024 | tf_op jit(solution)/shard_map/weigh/pallas_call | solution.py:25
  208.6 20.0 %unattend.3.grads.g1 = bf16[3,1024,384]{2,1,0:T(8,128)(2,1)} custom-call(s32[2]{0:T(128)} %pad_add_fusion.me_ref.at_ref, bf16[1024,768]{1,0:T(8,128)(2,1)} %get-tuple-element.283.query, bf16[1024,768]{1,0:T(8,128)(2,1)} %get-tuple-element.284.key, bf16[1024,768]{1,0:T(8,128)(2,1)} %get-tuple-element.285.value, bf16[1024,768]{1,0:T(8,128)(2,1)} %get-tuple-element.291.mixed, ...), custom_call_target="tpu_custom_call" | custom-call | flops 1024 | bytes 1024 | tf_op jit(solution)/shard_map/unattend/pallas_call | solution.py:25
  228.5 2.6 two.4
  232.2 6.2 %all-to-all-start.3 = ((bf16[8,96,768]{2,1,0:T(8,128)(2,1)}), bf16[8,96,768]{2,1,0:T(8,128)(2,1)S(1)}, u32[]{:S(2)}, u32[]{:S(2)}) async-start(bf16[8,96,768]{2,1,0:T(8,128)(2,1)} %bitcast.63), calls=%async_computation.3 | async-start | bytes 2359296 | tf_op jit(solution)/shard_map/all_to_all | solution.py:843
  239.5 7.4 %weigh.3 = (bf16[2,192,1152]{2,1,0:T(8,128)(2,1)}, bf16[2,192,1152]{2,1,0:T(8,128)(2,1)}, bf16[192,1920]{1,0:T(8,128)(2,1)}, bf16[192,1920]{1,0:T(8,128)(2,1)}) custom-call(s32[2]{0:T(128)} %pad_add_fusion.me_ref.at_ref, bf16[768,1024]{1,0:T(8,128)(2,1)} %get-tuple-element.279.turned, bf16[3,1024,384]{2,1,0:T(8,128)(2,1)} %unattend.3.grads.g1, ...), custom_call_target="tpu_custom_call" | custom-call | flops 1024 | bytes 1024 | tf_op jit(solution)/shard_map/weigh/pallas_call | solution.py:25
  248.0 2.1 add.110.first
  251.0 2.0 other.3
  255.2 2.4 collective-permute-start.19
  257.8 12.4 %unproject.1 = (bf16[256,768]{1,0:T(8,128)(2,1)}, bf16[256,768]{1,0:T(8,128)(2,1)}, bf16[256,768]{1,0:T(8,128)(2,1)}, bf16[256,768]{1,0:T(8,128)(2,1)}, f32[8,768]{1,0:T(8,128)}) custom-call(s32[2]{0:T(128)} %pad_add_fusion.me_ref.at_ref, bf16[3,1024,384]{2,1,0:T(8,128)(2,1)} %get-tuple-element.348.grads.g0, bf16[3,1024,384]{2,1,0:T(8,128)(2,1)} %unattend.3.grads.g1, ...), custom_call_target="tpu_custom_call" | custom-call | flops 1024 | bytes 1024 | tf_op jit(solution)/shard_map/unproject/pallas_call | solution.py:25
  273.7 2.6 collective-permute-start.24
  277.1 2.9 beside.1
  281.4 2.1 add.111.first
  285.3 1.9 collective-permute-start.23
  289.1 1.9 join.5
  295.3 2.1 two.5
  297.6 5.1 %all-to-all-start.4 = ((bf16[4,24,3072]{2,1,0:T(8,128)(2,1)}), bf16[4,24,3072]{2,1,0:T(8,128)(2,1)S(1)}, u32[]{:S(2)}, u32[]{:S(2)}) async-start(bf16[4,24,3072]{2,1,0:T(8,128)(2,1)} %bitcast.70), calls=%async_computation.4 | async-start | bytes 1179648 | tf_op jit(solution)/shard_map/all_to_all | solution.py:843
  304.9 1.7 join.6
  309.3 6.2 %all-to-all-done.4.parts = bf16[4,24,3072]{2,1,0:T(8,128)(2,1)S(1)} async-done(((bf16[4,24,3072]{2,1,0:T(8,128)(2,1)}), bf16[4,24,3072]{2,1,0:T(8,128)(2,1)S(1)}, u32[]{:S(2)}, u32[]{:S(2)}) %all-to-all-start.4) | async-done | bytes 589856 | tf_op jit(solution)/shard_map/all_to_all | solution.py:843
  315.5 7.3 %collective-permute-done.34.refs_1_ = bf16[384,768]{1,0:T(8,128)(2,1)S(1)} collective-permute-done((bf16[384,768]{1,0:T(8,128)(2,1)S(1)}, bf16[384,768]{1,0:T(8,128)(2,1)S(1)}, u32[]{:S(2)}, u32[]{:S(2)}) %collective-permute-start.34) | collective-permute-done | bytes 589856 | tf_op jit(solution)/shard_map/ppermute | solution.py:717
  322.9 2.6 terms.1
  325.5 5.1 %all-to-all-start.5 = ((bf16[4,32,3072]{2,1,0:T(8,128)(2,1)}), bf16[4,32,3072]{2,1,0:T(8,128)(2,1)S(1)}, u32[]{:S(2)}, u32[]{:S(2)}) async-start(bf16[4,32,3072]{2,1,0:T(8,128)(2,1)} %terms.1), calls=%async_computation.5 | async-start | bytes 1572864 | tf_op jit(solution)/shard_map/all_to_all | solution.py:843
  330.6 1.9 join.7
  334.0 3.3 lay.3
  337.3 9.9 %collective-permute-done.39.refs_3_ = bf16[384,768]{1,0:T(8,128)(2,1)S(1)} collective-permute-done((bf16[384,768]{1,0:T(8,128)(2,1)}, bf16[384,768]{1,0:T(8,128)(2,1)S(1)}, u32[]{:S(2)}, u32[]{:S(2)}) %collective-permute-start.39) | collective-permute-done | bytes 589856 | tf_op jit(solution)/shard_map/ppermute | solution.py:717
  350.7 10.2 %collective-permute-done.29.refs_2_ = bf16[256,768]{1,0:T(8,128)(2,1)S(1)} collective-permute-done((bf16[256,768]{1,0:T(8,128)(2,1)}, bf16[256,768]{1,0:T(8,128)(2,1)S(1)}, u32[]{:S(2)}, u32[]{:S(2)}) %collective-permute-start.29) | collective-permute-done | bytes 393248 | tf_op jit(solution)/shard_map/ppermute | solution.py:717
  360.9 7.7 %collective-permute-done.30.refs_3_ = bf16[256,768]{1,0:T(8,128)(2,1)S(1)} collective-permute-done((bf16[256,768]{1,0:T(8,128)(2,1)}, bf16[256,768]{1,0:T(8,128)(2,1)S(1)}, u32[]{:S(2)}, u32[]{:S(2)}) %collective-permute-start.30) | collective-permute-done | bytes 393248 | tf_op jit(solution)/shard_map/ppermute | solution.py:717
  369.3 3.3 lay.2
  372.6 4.0 %settle.1 = (f32[768,768]{1,0:T(8,128)}, f32[192,3072]{1,0:T(8,128)}) custom-call(s32[1]{0:T(128)} %bitcast.8.at_ref, bf16[384,768]{1,0:T(8,128)(2,1)} %bitcast.56, bf16[384,768]{1,0:T(8,128)(2,1)} %copy-done.15, bf16[384,768]{1,0:T(8,128)(2,1)} %bitcast.59, bf16[384,768]{1,0:T(8,128)(2,1)} %copy-done.16), custom_call_target="tpu_custom_call" | custom-call | flops 1024 | bytes 1024 | tf_op jit(solution)/shard_map/settle/pallas_call | solution.py:25
  377.6 4.5 %finish.1 = (f32[192,2304]{1,0:T(8,128)}, f32[192,768]{1,0:T(8,128)}, f32[1152,128]{1,0:T(8,128)}, f32[1152]{0:T(1024)}, f32[768]{0:T(1024)}, /*index=5*/f32[192...) custom-call(s32[2]{0:T(128)} %pad_add_fusion.me_ref.at_ref, bf16[4,32,3072]{2,1,0:T(8,128)(2,1)} %copy-done.5, ...), custom_call_target="tpu_custom_call" | custom-call | flops 1024 | bytes 1024 | tf_op jit(solution)/shard_map/finish/pallas_call | solution.py:25
  (240 shorter events, 53.3 us)
Async XLA Ops:
  2.1 34.7 %collective-permute-start.4 = (bf16[2,384,768]{2,1,0:T(8,128)(2,1)S(1)}, bf16[2,384,768]{2,1,0:T(8,128)(2,1)}, u32[]{:S(2)}, u32[]{:S(2)}) collective-permute-start(bf16[2,384,768]{2,1,0:T(8,128)(2,1)S(1)} %pad_maximum_fusion.p0), channel_id=1, source_target_pairs={{0,1},{1,0},{2,3},{3,2},{4,5},{5,4},{6,7},{7,6},{8,9},{9,8},{10,11... | collective-permute-start | bytes 3538952 | tf_op jit(solution)/shard_map/ppermute | solution.py:717
  3.1 16.4 %collective-permute-start = (bf16[384,768]{1,0:T(8,128)(2,1)}, bf16[384,768]{1,0:T(8,128)(2,1)}, u32[]{:S(2)}, u32[]{:S(2)}) collective-permute-start(bf16[384,768]{1,0:T(8,128)(2,1)} %dynamic-slice_bitcast_fusion), channel_id=1, source_target_pairs={{0,2},{1,3},{2,0},{3,1},{4,6},{5,7},{6,4},{7,5},{8,10},{9,11},{10,... | collective-permute-start | bytes 1769480 | tf_op jit(solution)/shard_map/ppermute | solution.py:717
  5.2 15.9 %collective-permute-start.2 = (f32[5,1408]{1,0:T(8,128)S(1)}, f32[5,1408]{1,0:T(8,128)S(1)}, u32[]{:S(2)}, u32[]{:S(2)}) collective-permute-start(f32[5,1408]{1,0:T(8,128)S(1)} %pad_maximum_fusion.5), channel_id=1, source_target_pairs={{0,2},{1,3},{2,0},{3,1},{4,6},{5,7},{6,4},{7,5},{8,10},{9,11},{10,... | collective-permute-start | bytes 84488 | tf_op jit(solution)/shard_map/ppermute | solution.py:717
  5.8 31.0 %all-to-all-start = ((bf16[4,256,768]{2,1,0:T(8,128)(2,1)}), bf16[4,256,768]{2,1,0:T(8,128)(2,1)S(1)}, u32[]{:S(2)}, u32[]{:S(2)}) async-start(bf16[4,256,768]{2,1,0:T(8,128)(2,1)} %param.15), calls=%async_computation | async-start | bytes 3145728 | tf_op jit(solution)/shard_map/all_to_all | solution.py:976
  19.5 14.8 %collective-permute-start.1 = (bf16[384,768]{1,0:T(8,128)(2,1)}, bf16[384,768]{1,0:T(8,128)(2,1)}, u32[]{:S(2)}, u32[]{:S(2)}) collective-permute-start(bf16[384,768]{1,0:T(8,128)(2,1)} %collective-permute-done.p2), channel_id=1, source_target_pairs={{0,4},{4,0},{8,12},{12,8},{16,20},{20,16},{24,28},{28,24},{1,5},{5... | collective-permute-start | bytes 1769480 | tf_op jit(solution)/shard_map/ppermute | solution.py:717
  21.1 15.8 %collective-permute-start.5 = (bf16[384,768]{1,0:T(8,128)(2,1)}, bf16[384,768]{1,0:T(8,128)(2,1)}, u32[]{:S(2)}, u32[]{:S(2)}) collective-permute-start(bf16[384,768]{1,0:T(8,128)(2,1)} %collective-permute-done.p2), channel_id=1, source_target_pairs={{0,1},{1,0},{2,3},{3,2},{4,5},{5,4},{6,7},{7,6},{8,9},{9,8},{10,11... | collective-permute-start | bytes 1769480 | tf_op jit(solution)/shard_map/ppermute | solution.py:717
  21.1 7.6 %collective-permute-start.3 = (f32[2,5,1408]{2,1,0:T(8,128)S(1)}, f32[2,5,1408]{2,1,0:T(8,128)S(1)}, u32[]{:S(2)}, u32[]{:S(2)}) collective-permute-start(f32[2,5,1408]{2,1,0:T(8,128)S(1)} %pad_maximum_fusion.3), channel_id=1, source_target_pairs={{0,1},{1,0},{2,3},{3,2},{4,5},{5,4},{6,7},{7,6},{8,9},{9,8},{10,11... | collective-permute-start | bytes 168968 | tf_op jit(solution)/shard_map/ppermute | solution.py:717
  34.3 2.5 collective-permute-start.6
  36.9 39.1 %collective-permute-start.7 = (bf16[768,768]{1,0:T(8,128)(2,1)}, bf16[768,768]{1,0:T(8,128)(2,1)}, u32[]{:S(2)}, u32[]{:S(2)}) collective-permute-start(bf16[768,768]{1,0:T(8,128)(2,1)} %get-tuple-element.288.p0), channel_id=1, source_target_pairs={{0,2},{1,3},{2,0},{3,1},{4,6},{5,7},{6,4},{7,5},{8,10},{9,11},{10,... | collective-permute-start | bytes 3538952 | tf_op jit(solution)/shard_map/ppermute | solution.py:717
  40.3 44.6 %collective-permute-start.8 = (bf16[768,768]{1,0:T(8,128)(2,1)}, bf16[768,768]{1,0:T(8,128)(2,1)}, u32[]{:S(2)}, u32[]{:S(2)}) collective-permute-start(bf16[768,768]{1,0:T(8,128)(2,1)} %get-tuple-element.288.p0), channel_id=1, source_target_pairs={{0,1},{1,0},{2,3},{3,2},{4,5},{5,4},{6,7},{7,6},{8,9},{9,8},{10,11... | collective-permute-start | bytes 3538952 | tf_op jit(solution)/shard_map/ppermute | solution.py:717
  49.7 35.2 %all-to-all-start.1 = ((bf16[4,256,768]{2,1,0:T(8,128)(2,1)}), bf16[4,256,768]{2,1,0:T(8,128)(2,1)S(1)}, u32[]{:S(2)}, u32[]{:S(2)}) async-start(bf16[4,256,768]{2,1,0:T(8,128)(2,1)} %param.29), calls=%async_computation.1 | async-start | bytes 3145728 | tf_op jit(solution)/shard_map/all_to_all | solution.py:1031
  76.0 8.9 %collective-permute-start.9 = (bf16[768,768]{1,0:T(8,128)(2,1)}, bf16[768,768]{1,0:T(8,128)(2,1)}, u32[]{:S(2)}, u32[]{:S(2)}) collective-permute-start(bf16[768,768]{1,0:T(8,128)(2,1)} %collective-permute-done.7.p2), channel_id=1, source_target_pairs={{0,1},{1,0},{2,3},{3,2},{4,5},{5,4},{6,7},{7,6},{8,9},{9,8},{10,11... | collective-permute-start | bytes 3538952 | tf_op jit(solution)/shard_map/ppermute | solution.py:717
  76.6 8.4 %collective-permute-start.10 = (bf16[768,768]{1,0:T(8,128)(2,1)S(1)}, bf16[768,768]{1,0:T(8,128)(2,1)}, u32[]{:S(2)}, u32[]{:S(2)}) collective-permute-start(bf16[768,768]{1,0:T(8,128)(2,1)S(1)} %copy-done.13), channel_id=1, source_target_pairs={{0,1},{1,0},{2,3},{3,2},{4,5},{5,4},{6,7},{7,6},{8,9},{9,8},{10,11... | collective-permute-start | bytes 3538952 | tf_op jit(solution)/shard_map/ppermute | solution.py:717
  76.6 42.4 %collective-permute-start.11 = (bf16[768,768]{1,0:T(8,128)(2,1)S(1)}, bf16[768,768]{1,0:T(8,128)(2,1)}, u32[]{:S(2)}, u32[]{:S(2)}) collective-permute-start(bf16[768,768]{1,0:T(8,128)(2,1)S(1)} %copy-done.13), channel_id=1, source_target_pairs={{0,2},{1,3},{2,0},{3,1},{4,6},{5,7},{6,4},{7,5},{8,10},{9,11},{10,... | collective-permute-start | bytes 3538952 | tf_op jit(solution)/shard_map/ppermute | solution.py:717
  119.0 3.1 collective-permute-start.12
  119.1 32.1 %collective-permute-start.13 = (bf16[2,768,768]{2,1,0:T(8,128)(2,1)}, bf16[2,768,768]{2,1,0:T(8,128)(2,1)S(1)}, u32[]{:S(2)}, u32[]{:S(2)}) collective-permute-start(bf16[2,768,768]{2,1,0:T(8,128)(2,1)} %get-tuple-element.326), channel_id=1, source_target_pairs={{0,1},{1,0},{2,3},{3,2},{4,5},{5,4},{6,7},{7,6},{8,9},{9,8},{10,11... | collective-permute-start | bytes 7077896 | tf_op jit(solution)/shard_map/ppermute | solution.py:717
  151.2 16.6 %collective-permute-start.14 = (bf16[2,768,768]{2,1,0:T(8,128)(2,1)}, bf16[2,768,768]{2,1,0:T(8,128)(2,1)}, u32[]{:S(2)}, u32[]{:S(2)}) collective-permute-start(bf16[2,768,768]{2,1,0:T(8,128)(2,1)} %get-tuple-element.337), channel_id=1, source_target_pairs={{0,1},{1,0},{2,3},{3,2},{4,5},{5,4},{6,7},{7,6},{8,9},{9,8},{10,11... | collective-permute-start | bytes 7077896 | tf_op jit(solution)/shard_map/ppermute | solution.py:717
  156.3 33.1 %collective-permute-start.15 = (bf16[768,768]{1,0:T(8,128)(2,1)}, bf16[768,768]{1,0:T(8,128)(2,1)S(1)}, u32[]{:S(2)}, u32[]{:S(2)}) collective-permute-start(bf16[768,768]{1,0:T(8,128)(2,1)} %other.2), channel_id=1, source_target_pairs={{0,2},{1,3},{2,0},{3,1},{4,6},{5,7},{6,4},{7,5},{8,10},{9,11},{10,... | collective-permute-start | bytes 3538952 | tf_op jit(solution)/shard_map/ppermute | solution.py:717
  193.4 37.7 %all-to-all-start.2 = ((bf16[8,96,768]{2,1,0:T(8,128)(2,1)}), bf16[8,96,768]{2,1,0:T(8,128)(2,1)S(1)}, u32[]{:S(2)}, u32[]{:S(2)}) async-start(bf16[8,96,768]{2,1,0:T(8,128)(2,1)} %bitcast.64), calls=%async_computation.2 | async-start | bytes 2359296 | tf_op jit(solution)/shard_map/all_to_all | solution.py:843
  199.9 28.6 %collective-permute-start.16 = (bf16[768,768]{1,0:T(8,128)(2,1)}, bf16[768,768]{1,0:T(8,128)(2,1)}, u32[]{:S(2)}, u32[]{:S(2)}) collective-permute-start(bf16[768,768]{1,0:T(8,128)(2,1)} %get-tuple-element.354), channel_id=1, source_target_pairs={{0,2},{1,3},{2,0},{3,1},{4,6},{5,7},{6,4},{7,5},{8,10},{9,11},{10,... | collective-permute-start | bytes 3538952 | tf_op jit(solution)/shard_map/ppermute | solution.py:717
  208.5 29.9 %collective-permute-start.17 = (bf16[2,192,1920]{2,1,0:T(8,128)(2,1)}, bf16[2,192,1920]{2,1,0:T(8,128)(2,1)S(1)}, u32[]{:S(2)}, u32[]{:S(2)}) collective-permute-start(bf16[2,192,1920]{2,1,0:T(8,128)(2,1)} %get-tuple-element.360), channel_id=1, source_target_pairs={{0,1},{1,0},{2,3},{3,2},{4,5},{5,4},{6,7},{7,6},{8,9},{9,8},{10,11... | collective-permute-start | bytes 4423688 | tf_op jit(solution)/shard_map/ppermute | solution.py:717
  232.2 44.1 %all-to-all-start.3 = ((bf16[8,96,768]{2,1,0:T(8,128)(2,1)}), bf16[8,96,768]{2,1,0:T(8,128)(2,1)S(1)}, u32[]{:S(2)}, u32[]{:S(2)}) async-start(bf16[8,96,768]{2,1,0:T(8,128)(2,1)} %bitcast.63), calls=%async_computation.3 | async-start | bytes 2359296 | tf_op jit(solution)/shard_map/all_to_all | solution.py:843
  247.0 3.1 collective-permute-start.18
  247.1 29.2 %collective-permute-start.20 = (bf16[192,1920]{1,0:T(8,128)(2,1)}, bf16[192,1920]{1,0:T(8,128)(2,1)}, u32[]{:S(2)}, u32[]{:S(2)}) collective-permute-start(bf16[192,1920]{1,0:T(8,128)(2,1)} %get-tuple-element.394), channel_id=1, source_target_pairs={{0,2},{1,3},{2,0},{3,1},{4,6},{5,7},{6,4},{7,5},{8,10},{9,11},{10,... | collective-permute-start | bytes 2211848 | tf_op jit(solution)/shard_map/ppermute | solution.py:717
  253.0 23.3 %collective-permute-start.21 = (bf16[192,1152]{1,0:T(8,128)(2,1)}, bf16[192,1152]{1,0:T(8,128)(2,1)S(1)}, u32[]{:S(2)}, u32[]{:S(2)}) collective-permute-start(bf16[192,1152]{1,0:T(8,128)(2,1)} %other.3), channel_id=1, source_target_pairs={{0,2},{1,3},{2,0},{3,1},{4,6},{5,7},{6,4},{7,5},{8,10},{9,11},{10,... | collective-permute-start | bytes 1327112 | tf_op jit(solution)/shard_map/ppermute | solution.py:717
  255.2 16.1 %collective-permute-start.19 = (bf16[96,768]{1,0:T(8,128)(2,1)S(1)}, bf16[96,768]{1,0:T(8,128)(2,1)S(1)}, u32[]{:S(2)}, u32[]{:S(2)}) collective-permute-start(bf16[96,768]{1,0:T(8,128)(2,1)S(1)} %copy-done.28), channel_id=1, source_target_pairs={{0,16},{4,20},{8,24},{12,28},{16,0},{20,4},{24,8},{28,12},{1,17},{... | collective-permute-start | bytes 442376 | tf_op jit(solution)/shard_map/ppermute | solution.py:717
  273.7 14.3 %collective-permute-start.24 = (bf16[192,768]{1,0:T(8,128)(2,1)}, bf16[192,768]{1,0:T(8,128)(2,1)S(1)}, u32[]{:S(2)}, u32[]{:S(2)}) collective-permute-start(bf16[192,768]{1,0:T(8,128)(2,1)} %bitcast.65), channel_id=1, source_target_pairs={{0,8},{4,12},{8,0},{12,4},{16,24},{20,28},{24,16},{28,20},{1,9},{5... | collective-permute-start | bytes 884744 | tf_op jit(solution)/shard_map/ppermute | solution.py:717
  280.0 14.6 %collective-permute-start.22 = (bf16[96,3072]{1,0:T(8,128)(2,1)}, bf16[96,3072]{1,0:T(8,128)(2,1)S(1)}, u32[]{:S(2)}, u32[]{:S(2)}) collective-permute-start(bf16[96,3072]{1,0:T(8,128)(2,1)} %get-tuple-element.408), channel_id=1, source_target_pairs={{0,4},{4,0},{8,12},{12,8},{16,20},{20,16},{24,28},{28,24},{1,5},{5... | collective-permute-start | bytes 1769480 | tf_op jit(solution)/shard_map/ppermute | solution.py:717
  285.3 9.2 %collective-permute-start.23 = (bf16[96,768]{1,0:T(8,128)(2,1)}, bf16[96,768]{1,0:T(8,128)(2,1)S(1)}, u32[]{:S(2)}, u32[]{:S(2)}) collective-permute-start(bf16[96,768]{1,0:T(8,128)(2,1)} %add.111.first), channel_id=1, source_target_pairs={{0,16},{4,20},{8,24},{12,28},{16,0},{20,4},{24,8},{28,12},{1,17},{... | collective-permute-start | bytes 442376 | tf_op jit(solution)/shard_map/ppermute | solution.py:717
  287.2 3.8 collective-permute-start.25
  287.2 3.8 collective-permute-start.26
  288.0 3.1 collective-permute-start.27
  291.1 31.7 %collective-permute-start.36 = (bf16[256,768]{1,0:T(8,128)(2,1)}, bf16[256,768]{1,0:T(8,128)(2,1)S(1)}, u32[]{:S(2)}, u32[]{:S(2)}) collective-permute-start(bf16[256,768]{1,0:T(8,128)(2,1)} %get-tuple-element.460), channel_id=1, source_target_pairs={{0,1},{1,0},{2,3},{3,2},{4,5},{5,4},{6,7},{7,6},{8,9},{9,8},{10,11... | collective-permute-start | bytes 1179656 | tf_op jit(solution)/shard_map/ppermute | solution.py:717
  291.7 31.2 %collective-permute-start.37 = (bf16[256,768]{1,0:T(8,128)(2,1)}, bf16[256,768]{1,0:T(8,128)(2,1)S(1)}, u32[]{:S(2)}, u32[]{:S(2)}) collective-permute-start(bf16[256,768]{1,0:T(8,128)(2,1)} %get-tuple-element.461), channel_id=1, source_target_pairs={{0,2},{1,3},{2,0},{3,1},{4,6},{5,7},{6,4},{7,5},{8,10},{9,11},{10,... | collective-permute-start | bytes 1179656 | tf_op jit(solution)/shard_map/ppermute | solution.py:717
  297.6 18.0 %all-to-all-start.4 = ((bf16[4,24,3072]{2,1,0:T(8,128)(2,1)}), bf16[4,24,3072]{2,1,0:T(8,128)(2,1)S(1)}, u32[]{:S(2)}, u32[]{:S(2)}) async-start(bf16[4,24,3072]{2,1,0:T(8,128)(2,1)} %bitcast.70), calls=%async_computation.4 | async-start | bytes 1179648 | tf_op jit(solution)/shard_map/all_to_all | solution.py:843
  302.9 3.7 collective-permute-start.33
  303.0 4.1 %collective-permute-start.32 = (f32[4,128]{1,0:T(4,128)S(1)}, f32[4,128]{1,0:T(4,128)S(1)}, u32[]{:S(2)}, u32[]{:S(2)}) collective-permute-start(f32[4,128]{1,0:T(4,128)S(1)} %fusion.13), channel_id=1, source_target_pairs={{0,2},{1,3},{2,0},{3,1},{4,6},{5,7},{6,4},{7,5},{8,10},{9,11},{10,... | collective-permute-start | bytes 6152 | tf_op jit(solution)/shard_map/ppermute | solution.py:717
  303.9 4.7 %collective-permute-start.31 = (f32[4,128]{1,0:T(4,128)S(1)}, f32[4,128]{1,0:T(4,128)S(1)}, u32[]{:S(2)}, u32[]{:S(2)}) collective-permute-start(f32[4,128]{1,0:T(4,128)S(1)} %fusion.13), channel_id=1, source_target_pairs={{0,1},{1,0},{2,3},{3,2},{4,5},{5,4},{6,7},{7,6},{8,9},{9,8},{10,11... | collective-permute-start | bytes 6152 | tf_op jit(solution)/shard_map/ppermute | solution.py:717
  306.6 16.2 %collective-permute-start.38 = (bf16[256,768]{1,0:T(8,128)(2,1)}, bf16[256,768]{1,0:T(8,128)(2,1)S(1)}, u32[]{:S(2)}, u32[]{:S(2)}) collective-permute-start(bf16[256,768]{1,0:T(8,128)(2,1)} %get-tuple-element.462), channel_id=1, source_target_pairs={{0,3},{1,2},{2,1},{3,0},{4,7},{5,6},{6,5},{7,4},{8,11},{9,10},{10,... | collective-permute-start | bytes 1179656 | tf_op jit(solution)/shard_map/ppermute | solution.py:717
  307.1 15.7 %collective-permute-start.34 = (bf16[384,768]{1,0:T(8,128)(2,1)S(1)}, bf16[384,768]{1,0:T(8,128)(2,1)S(1)}, u32[]{:S(2)}, u32[]{:S(2)}) collective-permute-start(bf16[384,768]{1,0:T(8,128)(2,1)S(1)} %bitcast.57), channel_id=1, source_target_pairs={{0,4},{4,0},{8,12},{12,8},{16,20},{20,16},{24,28},{28,24},{1,5},{5... | collective-permute-start | bytes 1769480 | tf_op jit(solution)/shard_map/ppermute | solution.py:717
  308.6 14.3 %collective-permute-start.35 = (bf16[192,768]{1,0:T(8,128)(2,1)}, bf16[192,768]{1,0:T(8,128)(2,1)S(1)}, u32[]{:S(2)}, u32[]{:S(2)}) collective-permute-start(bf16[192,768]{1,0:T(8,128)(2,1)} %bitcast.67), channel_id=1, source_target_pairs={{0,8},{4,12},{8,0},{12,4},{16,24},{20,28},{24,16},{28,20},{1,9},{5... | collective-permute-start | bytes 884744 | tf_op jit(solution)/shard_map/ppermute | solution.py:717
  325.5 21.8 %all-to-all-start.5 = ((bf16[4,32,3072]{2,1,0:T(8,128)(2,1)}), bf16[4,32,3072]{2,1,0:T(8,128)(2,1)S(1)}, u32[]{:S(2)}, u32[]{:S(2)}) async-start(bf16[4,32,3072]{2,1,0:T(8,128)(2,1)} %terms.1), calls=%async_computation.5 | async-start | bytes 1572864 | tf_op jit(solution)/shard_map/all_to_all | solution.py:843
  332.5 14.7 %collective-permute-start.39 = (bf16[384,768]{1,0:T(8,128)(2,1)}, bf16[384,768]{1,0:T(8,128)(2,1)S(1)}, u32[]{:S(2)}, u32[]{:S(2)}) collective-permute-start(bf16[384,768]{1,0:T(8,128)(2,1)} %bitcast.58), channel_id=1, source_target_pairs={{0,4},{4,0},{8,12},{12,8},{16,20},{20,16},{24,28},{28,24},{1,5},{5... | collective-permute-start | bytes 1769480 | tf_op jit(solution)/shard_map/ppermute | solution.py:717
  347.2 25.4 %copy-start.16 = (bf16[384,768]{1,0:T(8,128)(2,1)}, bf16[384,768]{1,0:T(8,128)(2,1)S(1)}, u32[]{:S(2)}) copy-start(bf16[384,768]{1,0:T(8,128)(2,1)S(1)} %collective-permute-done.39.refs_3_) | copy-start | bytes 1769476
  347.3 29.3 %collective-permute-start.40 = (bf16[4,32,3072]{2,1,0:T(8,128)(2,1)S(1)}, bf16[4,32,3072]{2,1,0:T(8,128)(2,1)S(1)}, u32[]{:S(2)}, u32[]{:S(2)}) collective-permute-start(bf16[4,32,3072]{2,1,0:T(8,128)(2,1)S(1)} %all-to-all-done.5.parts), channel_id=1, source_target_pairs={{0,4},{4,0},{8,12},{12,8},{16,20},{20,16},{24,28},{28,24},{1,5},{5... | collective-permute-start | bytes 2359304 | tf_op jit(solution)/shard_map/ppermute | solution.py:717
  348.8 1.9 collective-permute-start.28
  348.8 12.1 %collective-permute-start.29 = (bf16[256,768]{1,0:T(8,128)(2,1)}, bf16[256,768]{1,0:T(8,128)(2,1)S(1)}, u32[]{:S(2)}, u32[]{:S(2)}) collective-permute-start(bf16[256,768]{1,0:T(8,128)(2,1)} %get-tuple-element.446), channel_id=1, source_target_pairs={{0,2},{1,3},{2,0},{3,1},{4,6},{5,7},{6,4},{7,5},{8,10},{9,11},{10,... | collective-permute-start | bytes 1179656 | tf_op jit(solution)/shard_map/ppermute | solution.py:717
  350.0 18.5 %collective-permute-start.30 = (bf16[256,768]{1,0:T(8,128)(2,1)}, bf16[256,768]{1,0:T(8,128)(2,1)S(1)}, u32[]{:S(2)}, u32[]{:S(2)}) collective-permute-start(bf16[256,768]{1,0:T(8,128)(2,1)} %get-tuple-element.447), channel_id=1, source_target_pairs={{0,3},{1,2},{2,1},{3,0},{4,7},{5,6},{6,5},{7,4},{8,11},{9,10},{10,... | collective-permute-start | bytes 1179656 | tf_op jit(solution)/shard_map/ppermute | solution.py:717
  (43 other events, 226.3 us)
